TPU v7x, 256 devices: a whole 4x4x8 slice. The times are simulated.
256 devices in a mesh: blk: 32 (over x, z), uly: 8 (over y, core).
Axes of the slice: x: 4, y: 4, z: 8, core: 2. Of those that a mesh axis runs over, the one named last changes fastest.
Arguments:
- tokens: bfloat16 [12288, 3072], P(('blk', 'uly')), may hold values from -6 to 6
- mod_shift: float32 [3072], replicated, may hold values from -3 to 3
- mod_scale: float32 [3072], replicated, may hold values from -2 to 6
- out_gate: float32 [3072], replicated, may hold values from 0.5 to 1.5
- w_qkv: bfloat16 [3072, 24, 384], P(None, 'uly'), may hold values from -0.109375 to 0.109375
- w_out: bfloat16 [3072, 3072], P('uly'), may hold values from -0.109375 to 0.109375
- tile_map: int32 [32], replicated, may hold values from 0 to 31, as said below
- window_corner: int32 [32, 2], replicated, may hold values from 0 to 5, as said below
Outputs:
- mixed: bfloat16 [12288, 3072], P(('blk', 'uly'))
Inputs may be any that keep to these rules, and one draw needn't show every extreme that they name: `tile_map`: A permutation of the tile positions; position j holds a grid tile whose number differs from j by at most 1. `window_corner`: each query tile's 3 x 3 window lies inside the grid and contains the grid tile that its own position holds.
All inputs are finite; a program needn't handle non-finite values.
Results may differ from a plain program's by a relative error of at most 0.02.
The roundings to bfloat16 on the way count: a program that leaves them out, or rounds other values in their place, can miss the bound.
Values may be sent and summed in bfloat16 or wider, within the bound.
A program may use at most 128 MiB of HBM per device.

v0:
```python
import jax
import jax.numpy as jnp
from jax import lax
from jax.sharding import PartitionSpec as P

TILE = 384
WIN = 3
GW = 4


def from_behind(block, axis, distance):
    devices = range(lax.axis_size(axis))
    route = [(i - distance, i) for i in devices if i - distance in devices]
    return lax.ppermute(block, axis, route)


def on_device(tokens, mod_shift, mod_scale, out_gate, w_qkv, w_out, tile_map, window_corner):
    values_in = tokens.astype(jnp.float32)
    mean_row = jnp.mean(values_in, axis=-1, keepdims=True)
    centred = values_in - mean_row
    variance = jnp.mean(centred * centred, axis=-1, keepdims=True)
    normed = (centred * lax.rsqrt(variance + 1e-06) * (1.0 + mod_scale) + mod_shift).astype(
        jnp.bfloat16
    )
    heads_dev = w_qkv.shape[1]
    head_dim = w_qkv.shape[2] // 3
    qkv = jnp.einsum(
        "td,dhe->the",
        lax.all_gather(normed, "uly", axis=0, tiled=True),
        w_qkv,
        preferred_element_type=jnp.float32,
    ).astype(jnp.bfloat16)
    group_rows = qkv.shape[0]
    tiles_here = group_rows // TILE
    all_tiles = tile_map.shape[0]
    queries = qkv[:, :, :head_dim]
    keyval = qkv[:, :, head_dim:]
    shard_idx = lax.axis_index("blk")
    n_blk = lax.axis_size("blk")
    first_tile = shard_idx * tiles_here
    query_corner = lax.dynamic_slice(window_corner, (first_tile, 0), (tiles_here, 2))
    softmax_factor = 1.0 / jnp.sqrt(jnp.float32(head_dim))

    def attend(running, kv_tile, key_tile, is_valid):
        safe_tile = jnp.clip(key_tile, 0, all_tiles - 1)
        key_grid = lax.dynamic_index_in_dim(tile_map, safe_tile, keepdims=False)
        row_gap = key_grid // GW - query_corner[:, 0]
        col_gap = key_grid % GW - query_corner[:, 1]
        inside = (row_gap >= 0) & (row_gap < WIN) & (col_gap >= 0) & (col_gap < WIN) & is_valid

        def compute(state):
            highest, total, accum = state
            row_ok = jnp.repeat(inside, TILE)[None, :, None]
            scores = (
                jnp.einsum(
                    "qhd,khd->hqk",
                    queries,
                    kv_tile[:, :, :head_dim],
                    preferred_element_type=jnp.float32,
                )
                * softmax_factor
            )
            scores = jnp.where(row_ok, scores, -1e30)
            new_high = jnp.maximum(highest, jnp.max(scores, axis=-1))
            probs = jnp.where(row_ok, jnp.exp(scores - new_high[:, :, None]), 0.0)
            factor = jnp.exp(highest - new_high)
            total = total * factor + jnp.sum(probs, axis=-1)
            weights = probs.astype(jnp.bfloat16)
            accum = accum * factor[:, :, None] + jnp.einsum(
                "hqk,khd->hqd",
                weights,
                kv_tile[:, :, head_dim:],
                preferred_element_type=jnp.float32,
            )
            return (new_high, total, accum)

        def keep(state):
            return state

        return lax.cond(jnp.any(inside), compute, keep, running)

    def attend_group(running, arrived, source):
        is_valid = (source >= 0) & (source < n_blk)
        running = attend(running, arrived, source * tiles_here + 0, is_valid)
        return running

    running = (
        jnp.full((heads_dev, group_rows), -1e30, jnp.float32),
        jnp.zeros((heads_dev, group_rows), jnp.float32),
        jnp.zeros((heads_dev, group_rows, head_dim), jnp.float32),
    )
    reach = min((2 * GW + 3 + tiles_here) // tiles_here, n_blk - 1)
    running = attend_group(running, keyval, shard_idx)
    for offset in range(-reach, reach + 1):
        if offset != 0:
            arrived = from_behind(keyval, "blk", offset)
            running = attend_group(running, arrived, shard_idx - offset)
    highest, total, accum = running
    attn = (accum / total[:, :, None]).astype(jnp.bfloat16)
    attn = jnp.transpose(attn, (1, 0, 2)).reshape(group_rows, heads_dev * head_dim)
    summed = lax.psum_scatter(
        jnp.dot(attn, w_out, preferred_element_type=jnp.float32).astype(jnp.bfloat16),
        "uly",
        scatter_dimension=0,
        tiled=True,
    ).astype(jnp.float32)
    return (out_gate * summed).astype(jnp.bfloat16)


def solution(mesh):
    in_specs = (
        P(("blk", "uly"), None),
        P(),
        P(),
        P(),
        P(None, "uly", None),
        P("uly", None),
        P(),
        P(),
    )
    out_specs = P(("blk", "uly"), None)
    return jax.shard_map(
        on_device, mesh=mesh, in_specs=in_specs, out_specs=out_specs, check_vma=False
    )
```

profile of v0, /device:TPU:1, one launch (start us, length us, event | category | flops | bytes accessed | tf_op | source)
XLA Modules:
  0.0 683.8 jit_solution(6186179026058369950)
XLA Ops:
  11.7 32.5 %all-gather.2.cloned.1.call-done = bf16[384,3072]{1,0:T(8,128)(2,1)} async-done(((bf16[48,3072]{1,0:T(8,128)(2,1)}), bf16[384,3072]{1,0:T(8,128)(2,1)}) %all-gather.2.cloned.1.call-update) | async-done | bytes 2359312 | tf_op jit(solution)/shard_map/all_gather | solution.py:29
  44.2 6.9 %fusion.378 = bf16[384,3,384]{2,0,1:T(8,128)(2,1)S(1)} fusion(bf16[3072,3,384]{2,0,1:T(8,128)(2,1)} %param.62, bf16[384,3072]{1,0:T(8,128)(2,1)} %all-gather.2.cloned.1.call-done), kind=kOutput, calls=%fused_computation.479 | convolution fusion | flops 2718351360 | bytes 10321920 | tf_op jit(solution)/shard_map/td,dhe->the/dot_general | solution.py:27
  59.4 23.6 %collective-permute-done = bf16[384,3,256]{2,0,1:T(8,128)(2,1)} collective-permute-done((bf16[384,3,256]{2,0,1:T(8,128)(2,1)}, bf16[384,3,256]{2,0,1:T(8,128)(2,1)}, u32[]{:S(2)}, u32[]{:S(2)}) %collective-permute-start) | collective-permute-done | bytes 589856 | tf_op jit(solution)/shard_map/ppermute | solution.py:14
  84.3 24.0 %collective-permute-done.1 = bf16[384,3,256]{2,0,1:T(8,128)(2,1)} collective-permute-done((bf16[384,3,256]{2,0,1:T(8,128)(2,1)}, bf16[384,3,256]{2,0,1:T(8,128)(2,1)}, u32[]{:S(2)}, u32[]{:S(2)}) %collective-permute-start.1) | collective-permute-done | bytes 589856 | tf_op jit(solution)/shard_map/ppermute | solution.py:14
  109.6 17.3 %collective-permute-done.2 = bf16[384,3,256]{2,0,1:T(8,128)(2,1)} collective-permute-done((bf16[384,3,256]{2,0,1:T(8,128)(2,1)}, bf16[384,3,256]{2,0,1:T(8,128)(2,1)}, u32[]{:S(2)}, u32[]{:S(2)}) %collective-permute-start.2) | collective-permute-done | bytes 589856 | tf_op jit(solution)/shard_map/ppermute | solution.py:14
  132.0 18.8 %collective-permute-done.6 = bf16[384,3,256]{2,0,1:T(8,128)(2,1)} collective-permute-done((bf16[384,3,256]{2,0,1:T(8,128)(2,1)}, bf16[384,3,256]{2,0,1:T(8,128)(2,1)}, u32[]{:S(2)}, u32[]{:S(2)}) %collective-permute-start.6) | collective-permute-done | bytes 589856 | tf_op jit(solution)/shard_map/ppermute | solution.py:14
  152.1 57.6 %collective-permute-start.12 = (bf16[384,3,256]{2,0,1:T(8,128)(2,1)}, bf16[384,3,256]{2,0,1:T(8,128)(2,1)}, u32[]{:S(2)}, u32[]{:S(2)}) collective-permute-start(bf16[384,3,256]{2,0,1:T(8,128)(2,1)} %slice.214), channel_id=1, source_target_pairs={{0,8},{8,16},{16,24},{24,32},{32,40},{40,48},{48,56},{56,64},{64,7... | collective-permute-start | bytes 1769480 | tf_op jit(solution)/shard_map/ppermute | solution.py:14
  209.8 17.8 %collective-permute-start.13 = (bf16[384,3,256]{2,0,1:T(8,128)(2,1)}, bf16[384,3,256]{2,0,1:T(8,128)(2,1)}, u32[]{:S(2)}, u32[]{:S(2)}) collective-permute-start(bf16[384,3,256]{2,0,1:T(8,128)(2,1)} %slice.214), channel_id=1, source_target_pairs={{0,16},{8,24},{16,32},{24,40},{32,48},{40,56},{48,64},{56,72},{64,... | collective-permute-start | bytes 1769480 | tf_op jit(solution)/shard_map/ppermute | solution.py:14
  227.6 6.4 collective-permute-start.14
  234.0 16.6 %collective-permute-start.15 = (bf16[384,3,256]{2,0,1:T(8,128)(2,1)}, bf16[384,3,256]{2,0,1:T(8,128)(2,1)}, u32[]{:S(2)}, u32[]{:S(2)}) collective-permute-start(bf16[384,3,256]{2,0,1:T(8,128)(2,1)} %slice.214), channel_id=1, source_target_pairs={{0,32},{8,40},{16,48},{24,56},{32,64},{40,72},{48,80},{56,88},{64,... | collective-permute-start | bytes 1769480 | tf_op jit(solution)/shard_map/ppermute | solution.py:14
  250.6 24.4 %collective-permute-start.16 = (bf16[384,3,256]{2,0,1:T(8,128)(2,1)}, bf16[384,3,256]{2,0,1:T(8,128)(2,1)}, u32[]{:S(2)}, u32[]{:S(2)}) collective-permute-start(bf16[384,3,256]{2,0,1:T(8,128)(2,1)} %slice.214), channel_id=1, source_target_pairs={{0,40},{8,48},{16,56},{24,64},{32,72},{40,80},{48,88},{56,96},{64,... | collective-permute-start | bytes 1769480 | tf_op jit(solution)/shard_map/ppermute | solution.py:14
  275.0 18.9 %collective-permute-start.17 = (bf16[384,3,256]{2,0,1:T(8,128)(2,1)}, bf16[384,3,256]{2,0,1:T(8,128)(2,1)}, u32[]{:S(2)}, u32[]{:S(2)}) collective-permute-start(bf16[384,3,256]{2,0,1:T(8,128)(2,1)} %slice.214), channel_id=1, source_target_pairs={{0,48},{8,56},{16,64},{24,72},{32,80},{40,88},{48,96},{56,104},{64... | collective-permute-start | bytes 1769480 | tf_op jit(solution)/shard_map/ppermute | solution.py:14
  293.9 82.4 %collective-permute-start.18 = (bf16[384,3,256]{2,0,1:T(8,128)(2,1)}, bf16[384,3,256]{2,0,1:T(8,128)(2,1)}, u32[]{:S(2)}, u32[]{:S(2)}) collective-permute-start(bf16[384,3,256]{2,0,1:T(8,128)(2,1)} %slice.214), channel_id=1, source_target_pairs={{0,56},{8,64},{16,72},{24,80},{32,88},{40,96},{48,104},{56,112},{6... | collective-permute-start | bytes 1769480 | tf_op jit(solution)/shard_map/ppermute | solution.py:14
  376.3 9.5 %collective-permute-start.19 = (bf16[384,3,256]{2,0,1:T(8,128)(2,1)}, bf16[384,3,256]{2,0,1:T(8,128)(2,1)}, u32[]{:S(2)}, u32[]{:S(2)}) collective-permute-start(bf16[384,3,256]{2,0,1:T(8,128)(2,1)} %slice.214), channel_id=1, source_target_pairs={{0,64},{8,72},{16,80},{24,88},{32,96},{40,104},{48,112},{56,120},{... | collective-permute-start | bytes 1769480 | tf_op jit(solution)/shard_map/ppermute | solution.py:14
  391.5 39.3 %collective-permute-start.22 = (bf16[384,3,256]{2,0,1:T(8,128)(2,1)}, bf16[384,3,256]{2,0,1:T(8,128)(2,1)}, u32[]{:S(2)}, u32[]{:S(2)}) collective-permute-start(bf16[384,3,256]{2,0,1:T(8,128)(2,1)} %slice.214), channel_id=1, source_target_pairs={{0,88},{8,96},{16,104},{24,112},{32,120},{40,128},{48,136},{56,144... | collective-permute-start | bytes 1769480 | tf_op jit(solution)/shard_map/ppermute | solution.py:14
  430.7 8.0 %collective-permute-start.23 = (bf16[384,3,256]{2,0,1:T(8,128)(2,1)}, bf16[384,3,256]{2,0,1:T(8,128)(2,1)}, u32[]{:S(2)}, u32[]{:S(2)}) collective-permute-start(bf16[384,3,256]{2,0,1:T(8,128)(2,1)} %slice.214), channel_id=1, source_target_pairs={{0,96},{8,104},{16,112},{24,120},{32,128},{40,136},{48,144},{56,15... | collective-permute-start | bytes 1769480 | tf_op jit(solution)/shard_map/ppermute | solution.py:14
  540.1 5.8 conditional.27
  545.9 5.6 conditional.28
  551.5 5.6 conditional.30
  557.1 5.6 conditional.31
  562.7 5.6 conditional.32
  568.3 5.6 conditional.33
  574.1 5.6 conditional.35
  594.3 80.8 %reduce-scatter.2.cloned.1.call-done = bf16[48,3072]{1,0:T(8,128)(2,1)} async-done(((bf16[384,3072]{1,0:T(8,128)(2,1)}), bf16[48,3072]{1,0:T(8,128)(2,1)}) %reduce-scatter.2.cloned.1.call-update) | async-done | bytes 294928 | tf_op jit(solution)/shard_map/reduce_scatter | solution.py:101
  (136 shorter events, 104.6 us)
Async XLA Ops:
  6.5 37.6 %all-gather.2.cloned.1.call-start = ((), (), s32[]{:S(2)}) async-start(), calls=%async_computation.1 | async-start | bytes 2654208 | tf_op jit(solution)/shard_map/all_gather | solution.py:29
  11.6 663.4 %reduce-scatter.2.cloned.1.call-start = ((), (), s32[]{:S(2)}) async-start(), calls=%async_computation.2 | async-start | bytes 2654208 | tf_op jit(solution)/shard_map/reduce_scatter | solution.py:101
  54.2 54.1 %collective-permute-start.1 = (bf16[384,3,256]{2,0,1:T(8,128)(2,1)}, bf16[384,3,256]{2,0,1:T(8,128)(2,1)}, u32[]{:S(2)}, u32[]{:S(2)}) collective-permute-start(bf16[384,3,256]{2,0,1:T(8,128)(2,1)} %slice.214), channel_id=1, source_target_pairs={{88,0},{96,8},{104,16},{112,24},{120,32},{128,40},{136,48},{144,56... | collective-permute-start | bytes 1769480 | tf_op jit(solution)/shard_map/ppermute | solution.py:14
  55.5 71.3 %collective-permute-start.2 = (bf16[384,3,256]{2,0,1:T(8,128)(2,1)}, bf16[384,3,256]{2,0,1:T(8,128)(2,1)}, u32[]{:S(2)}, u32[]{:S(2)}) collective-permute-start(bf16[384,3,256]{2,0,1:T(8,128)(2,1)} %slice.214), channel_id=1, source_target_pairs={{80,0},{88,8},{96,16},{104,24},{112,32},{120,40},{128,48},{136,56}... | collective-permute-start | bytes 1769480 | tf_op jit(solution)/shard_map/ppermute | solution.py:14
  56.8 71.3 %collective-permute-start.3 = (bf16[384,3,256]{2,0,1:T(8,128)(2,1)}, bf16[384,3,256]{2,0,1:T(8,128)(2,1)}, u32[]{:S(2)}, u32[]{:S(2)}) collective-permute-start(bf16[384,3,256]{2,0,1:T(8,128)(2,1)} %slice.214), channel_id=1, source_target_pairs={{72,0},{80,8},{88,16},{96,24},{104,32},{112,40},{120,48},{128,56},... | collective-permute-start | bytes 1769480 | tf_op jit(solution)/shard_map/ppermute | solution.py:14
  58.1 71.3 %collective-permute-start.4 = (bf16[384,3,256]{2,0,1:T(8,128)(2,1)}, bf16[384,3,256]{2,0,1:T(8,128)(2,1)}, u32[]{:S(2)}, u32[]{:S(2)}) collective-permute-start(bf16[384,3,256]{2,0,1:T(8,128)(2,1)} %slice.214), channel_id=1, source_target_pairs={{64,0},{72,8},{80,16},{88,24},{96,32},{104,40},{112,48},{120,56},{... | collective-permute-start | bytes 1769480 | tf_op jit(solution)/shard_map/ppermute | solution.py:14
  83.0 47.7 %collective-permute-start.5 = (bf16[384,3,256]{2,0,1:T(8,128)(2,1)}, bf16[384,3,256]{2,0,1:T(8,128)(2,1)}, u32[]{:S(2)}, u32[]{:S(2)}) collective-permute-start(bf16[384,3,256]{2,0,1:T(8,128)(2,1)} %slice.214), channel_id=1, source_target_pairs={{56,0},{64,8},{72,16},{80,24},{88,32},{96,40},{104,48},{112,56},{1... | collective-permute-start | bytes 1769480 | tf_op jit(solution)/shard_map/ppermute | solution.py:14
  108.3 42.6 %collective-permute-start.6 = (bf16[384,3,256]{2,0,1:T(8,128)(2,1)}, bf16[384,3,256]{2,0,1:T(8,128)(2,1)}, u32[]{:S(2)}, u32[]{:S(2)}) collective-permute-start(bf16[384,3,256]{2,0,1:T(8,128)(2,1)} %slice.214), channel_id=1, source_target_pairs={{48,0},{56,8},{64,16},{72,24},{80,32},{88,40},{96,48},{104,56},{11... | collective-permute-start | bytes 1769480 | tf_op jit(solution)/shard_map/ppermute | solution.py:14
  128.1 81.7 %collective-permute-start.8 = (bf16[384,3,256]{2,0,1:T(8,128)(2,1)}, bf16[384,3,256]{2,0,1:T(8,128)(2,1)}, u32[]{:S(2)}, u32[]{:S(2)}) collective-permute-start(bf16[384,3,256]{2,0,1:T(8,128)(2,1)} %slice.214), channel_id=1, source_target_pairs={{32,0},{40,8},{48,16},{56,24},{64,32},{72,40},{80,48},{88,56},{96,... | collective-permute-start | bytes 1769480 | tf_op jit(solution)/shard_map/ppermute | solution.py:14
  129.4 98.1 %collective-permute-start.9 = (bf16[384,3,256]{2,0,1:T(8,128)(2,1)}, bf16[384,3,256]{2,0,1:T(8,128)(2,1)}, u32[]{:S(2)}, u32[]{:S(2)}) collective-permute-start(bf16[384,3,256]{2,0,1:T(8,128)(2,1)} %slice.214), channel_id=1, source_target_pairs={{24,0},{32,8},{40,16},{48,24},{56,32},{64,40},{72,48},{80,56},{88,... | collective-permute-start | bytes 1769480 | tf_op jit(solution)/shard_map/ppermute | solution.py:14
  130.7 103.2 %collective-permute-start.10 = (bf16[384,3,256]{2,0,1:T(8,128)(2,1)}, bf16[384,3,256]{2,0,1:T(8,128)(2,1)}, u32[]{:S(2)}, u32[]{:S(2)}) collective-permute-start(bf16[384,3,256]{2,0,1:T(8,128)(2,1)} %slice.214), channel_id=1, source_target_pairs={{16,0},{24,8},{32,16},{40,24},{48,32},{56,40},{64,48},{72,56},{80,... | collective-permute-start | bytes 1769480 | tf_op jit(solution)/shard_map/ppermute | solution.py:14
  150.8 99.7 %collective-permute-start.11 = (bf16[384,3,256]{2,0,1:T(8,128)(2,1)}, bf16[384,3,256]{2,0,1:T(8,128)(2,1)}, u32[]{:S(2)}, u32[]{:S(2)}) collective-permute-start(bf16[384,3,256]{2,0,1:T(8,128)(2,1)} %slice.214), channel_id=1, source_target_pairs={{8,0},{16,8},{24,16},{32,24},{40,32},{48,40},{56,48},{64,56},{72,6... | collective-permute-start | bytes 1769480 | tf_op jit(solution)/shard_map/ppermute | solution.py:14
  152.1 122.9 %collective-permute-start.12 = (bf16[384,3,256]{2,0,1:T(8,128)(2,1)}, bf16[384,3,256]{2,0,1:T(8,128)(2,1)}, u32[]{:S(2)}, u32[]{:S(2)}) collective-permute-start(bf16[384,3,256]{2,0,1:T(8,128)(2,1)} %slice.214), channel_id=1, source_target_pairs={{0,8},{8,16},{16,24},{24,32},{32,40},{40,48},{48,56},{56,64},{64,7... | collective-permute-start | bytes 1769480 | tf_op jit(solution)/shard_map/ppermute | solution.py:14
  209.8 84.1 %collective-permute-start.13 = (bf16[384,3,256]{2,0,1:T(8,128)(2,1)}, bf16[384,3,256]{2,0,1:T(8,128)(2,1)}, u32[]{:S(2)}, u32[]{:S(2)}) collective-permute-start(bf16[384,3,256]{2,0,1:T(8,128)(2,1)} %slice.214), channel_id=1, source_target_pairs={{0,16},{8,24},{16,32},{24,40},{32,48},{40,56},{48,64},{56,72},{64,... | collective-permute-start | bytes 1769480 | tf_op jit(solution)/shard_map/ppermute | solution.py:14
  227.6 148.8 %collective-permute-start.14 = (bf16[384,3,256]{2,0,1:T(8,128)(2,1)}, bf16[384,3,256]{2,0,1:T(8,128)(2,1)}, u32[]{:S(2)}, u32[]{:S(2)}) collective-permute-start(bf16[384,3,256]{2,0,1:T(8,128)(2,1)} %slice.214), channel_id=1, source_target_pairs={{0,24},{8,32},{16,40},{24,48},{32,56},{40,64},{48,72},{56,80},{64,... | collective-permute-start | bytes 1769480 | tf_op jit(solution)/shard_map/ppermute | solution.py:14
  234.0 151.8 %collective-permute-start.15 = (bf16[384,3,256]{2,0,1:T(8,128)(2,1)}, bf16[384,3,256]{2,0,1:T(8,128)(2,1)}, u32[]{:S(2)}, u32[]{:S(2)}) collective-permute-start(bf16[384,3,256]{2,0,1:T(8,128)(2,1)} %slice.214), channel_id=1, source_target_pairs={{0,32},{8,40},{16,48},{24,56},{32,64},{40,72},{48,80},{56,88},{64,... | collective-permute-start | bytes 1769480 | tf_op jit(solution)/shard_map/ppermute | solution.py:14
  250.6 138.1 %collective-permute-start.16 = (bf16[384,3,256]{2,0,1:T(8,128)(2,1)}, bf16[384,3,256]{2,0,1:T(8,128)(2,1)}, u32[]{:S(2)}, u32[]{:S(2)}) collective-permute-start(bf16[384,3,256]{2,0,1:T(8,128)(2,1)} %slice.214), channel_id=1, source_target_pairs={{0,40},{8,48},{16,56},{24,64},{32,72},{40,80},{48,88},{56,96},{64,... | collective-permute-start | bytes 1769480 | tf_op jit(solution)/shard_map/ppermute | solution.py:14
  275.0 116.5 %collective-permute-start.17 = (bf16[384,3,256]{2,0,1:T(8,128)(2,1)}, bf16[384,3,256]{2,0,1:T(8,128)(2,1)}, u32[]{:S(2)}, u32[]{:S(2)}) collective-permute-start(bf16[384,3,256]{2,0,1:T(8,128)(2,1)} %slice.214), channel_id=1, source_target_pairs={{0,48},{8,56},{16,64},{24,72},{32,80},{40,88},{48,96},{56,104},{64... | collective-permute-start | bytes 1769480 | tf_op jit(solution)/shard_map/ppermute | solution.py:14
  293.9 136.8 %collective-permute-start.18 = (bf16[384,3,256]{2,0,1:T(8,128)(2,1)}, bf16[384,3,256]{2,0,1:T(8,128)(2,1)}, u32[]{:S(2)}, u32[]{:S(2)}) collective-permute-start(bf16[384,3,256]{2,0,1:T(8,128)(2,1)} %slice.214), channel_id=1, source_target_pairs={{0,56},{8,64},{16,72},{24,80},{32,88},{40,96},{48,104},{56,112},{6... | collective-permute-start | bytes 1769480 | tf_op jit(solution)/shard_map/ppermute | solution.py:14
  376.3 210.8 %collective-permute-start.19 = (bf16[384,3,256]{2,0,1:T(8,128)(2,1)}, bf16[384,3,256]{2,0,1:T(8,128)(2,1)}, u32[]{:S(2)}, u32[]{:S(2)}) collective-permute-start(bf16[384,3,256]{2,0,1:T(8,128)(2,1)} %slice.214), channel_id=1, source_target_pairs={{0,64},{8,72},{16,80},{24,88},{32,96},{40,104},{48,112},{56,120},{... | collective-permute-start | bytes 1769480 | tf_op jit(solution)/shard_map/ppermute | solution.py:14
  385.8 201.4 %collective-permute-start.20 = (bf16[384,3,256]{2,0,1:T(8,128)(2,1)}, bf16[384,3,256]{2,0,1:T(8,128)(2,1)}, u32[]{:S(2)}, u32[]{:S(2)}) collective-permute-start(bf16[384,3,256]{2,0,1:T(8,128)(2,1)} %slice.214), channel_id=1, source_target_pairs={{0,72},{8,80},{16,88},{24,96},{32,104},{40,112},{48,120},{56,128},... | collective-permute-start | bytes 1769480 | tf_op jit(solution)/shard_map/ppermute | solution.py:14
  388.6 198.5 %collective-permute-start.21 = (bf16[384,3,256]{2,0,1:T(8,128)(2,1)}, bf16[384,3,256]{2,0,1:T(8,128)(2,1)}, u32[]{:S(2)}, u32[]{:S(2)}) collective-permute-start(bf16[384,3,256]{2,0,1:T(8,128)(2,1)} %slice.214), channel_id=1, source_target_pairs={{0,80},{8,88},{16,96},{24,104},{32,112},{40,120},{48,128},{56,136}... | collective-permute-start | bytes 1769480 | tf_op jit(solution)/shard_map/ppermute | solution.py:14
  391.5 195.7 %collective-permute-start.22 = (bf16[384,3,256]{2,0,1:T(8,128)(2,1)}, bf16[384,3,256]{2,0,1:T(8,128)(2,1)}, u32[]{:S(2)}, u32[]{:S(2)}) collective-permute-start(bf16[384,3,256]{2,0,1:T(8,128)(2,1)} %slice.214), channel_id=1, source_target_pairs={{0,88},{8,96},{16,104},{24,112},{32,120},{40,128},{48,136},{56,144... | collective-permute-start | bytes 1769480 | tf_op jit(solution)/shard_map/ppermute | solution.py:14
  430.7 160.3 %collective-permute-start.23 = (bf16[384,3,256]{2,0,1:T(8,128)(2,1)}, bf16[384,3,256]{2,0,1:T(8,128)(2,1)}, u32[]{:S(2)}, u32[]{:S(2)}) collective-permute-start(bf16[384,3,256]{2,0,1:T(8,128)(2,1)} %slice.214), channel_id=1, source_target_pairs={{0,96},{8,104},{16,112},{24,120},{32,128},{40,136},{48,144},{56,15... | collective-permute-start | bytes 1769480 | tf_op jit(solution)/shard_map/ppermute | solution.py:14
  (7 other events, 1579.4 us)
Sparse Core Ops, SparseCore 0:
  11.7 32.3 all-gather.1
  594.4 80.6 reduce-scatter.1
where the time goes:
time: 697 us; the launch traced here: 684 us
  starting transfers between devices  302 us (43%)
  waiting for transfers between devices  197 us (28%)
  between operations  107 us (15%)
  matrix products  38 us (5%)
  other arithmetic  23.9 us (3%)
  local copies, waits for them, and re-layouts  11.1 us (2%)
    ppermute x24, starting transfers between devices, from_behind(): return lax.ppermute(block, axis, route)  302 us
    ppermute x24, waiting for transfers between devices, from_behind(): return lax.ppermute(block, axis, route)  83.7 us
    reduce_scatter x1, waiting for transfers between devices, on_device(): lax.psum_scatter(jnp.dot(attn, w_out, preferred_element_type=jnp.float32)...  80.8 us
    all_gather x1, waiting for transfers between devices, on_device(): lax.all_gather(normed, 'uly', axis=0, tiled=True)  32.5 us
    dot_general x9, matrix products, compute(): jnp.einsum('hqk,khd->hqd', weights, kv_tile[:, :, head_dim:], preferred_e...  15.8 us
  transfers between devices with their start and end apart: 26, of which 6 were waited for; matrix products, arithmetic and copies ran while one was open for 8% of the time, Pallas kernels for 0%

commit v1 on v0

v1 whole, which is shorter than its diff:
```python
import jax
import jax.numpy as jnp
from jax import lax
from jax.experimental import pallas as pl
from jax.experimental.pallas import tpu as pltpu
from jax.sharding import PartitionSpec as P

TILE = 384
WIN = 3
GW = 4
NX = 4
NZ = 8
NY = 4
HD = 128
MESH = pl.DeviceIdType.MESH
VMEM_LIMIT = 62 * 1024 * 1024


def push(src, dst, send_sem, recv_sem, blk, uly):
    return pltpu.make_async_remote_copy(
        src_ref=src,
        dst_ref=dst,
        send_sem=send_sem,
        recv_sem=recv_sem,
        device_id={"blk": blk, "uly": uly},
        device_id_type=MESH,
    )


def where_am_i():
    blk = lax.axis_index("blk")
    uly = lax.axis_index("uly")
    return blk, uly


def greet(peers):
    barrier = pltpu.get_barrier_semaphore()
    for blk, uly in peers:
        pl.semaphore_signal(
            barrier, inc=1, device_id={"blk": blk, "uly": uly}, device_id_type=MESH
        )
    pl.semaphore_wait(barrier, len(peers))


def project_kernel(x_ref, shift_ref, scale_ref, w_hbm, qkv_ref, xbuf, wbuf, wsem, ssem, rsem):
    blk, uly = where_am_i()
    y, c = uly // 2, uly % 2
    rows = x_ref.shape[0]
    half = x_ref.shape[1] // 2
    heads = w_hbm.shape[0]
    for h in range(heads):
        pltpu.make_async_copy(w_hbm.at[h], wbuf.at[h], wsem.at[h]).start()

    up = ((y + 1) % NY) * 2 + c
    dn = ((y + 3) % NY) * 2 + c
    opp = ((y + 2) % NY) * 2 + c
    mate = y * 2 + (1 - c)
    greet([(blk, up), (blk, dn), (blk, mate)])

    values = x_ref[...].astype(jnp.float32)
    mean = jnp.mean(values, axis=-1, keepdims=True)
    centred = values - mean
    var = jnp.mean(centred * centred, axis=-1, keepdims=True)
    normed = centred * lax.rsqrt(var + 1e-06) * (1.0 + scale_ref[...]) + shift_ref[...]

    def piece(u, k):
        return xbuf.at[pl.ds(pl.multiple_of(u * rows, 16), rows), pl.ds(k * half, half)]

    xbuf[pl.ds(pl.multiple_of(uly * rows, 16), rows), :] = normed.astype(xbuf.dtype)

    sent = []

    def send(u, k, to):
        copy = push(piece(u, k), piece(u, k), ssem.at[len(sent)], rsem.at[u, k], blk, to)
        copy.start()
        sent.append(copy)

    def arrive(u, k):
        push(piece(u, k), piece(u, k), ssem.at[0], rsem.at[u, k], blk, mate).wait_recv()

    for first in (0, 1):
        send(uly, first, up)
        send(uly, 1 - first, dn)
        send(uly, first, mate)
    arrive(dn, 0)
    send(dn, 0, up)
    send(dn, 0, mate)
    arrive(up, 1)
    send(up, 1, dn)
    send(up, 1, mate)
    arrive(dn, 1)
    send(dn, 1, mate)
    arrive(up, 0)
    send(up, 0, mate)
    arrive(opp, 0)
    send(opp, 0, mate)
    arrive(opp, 1)
    send(opp, 1, mate)
    for k in (0, 1):
        for step in range(NY):
            arrive(((y + step) % NY) * 2 + (1 - c), k)

    for h in range(heads):
        pltpu.make_async_copy(w_hbm.at[h], wbuf.at[h], wsem.at[h]).wait()
        result = jnp.dot(xbuf[...], wbuf[h], preferred_element_type=jnp.float32)
        for part in range(3):
            qkv_ref[h, part] = result[:, part * HD : (part + 1) * HD].astype(qkv_ref.dtype)
    for copy in sent:
        copy.wait_send()


def attend_kernel(
    map_ref, corner_ref, qkv_hbm, attn_ref,
    kv, qb, ob, back, scores, asem, qsem, kvsem, bsem, hsem, osem,
):
    blk, uly = where_am_i()
    y, c = uly // 2, uly % 2
    x, z = blk // NZ, blk % NZ
    line = x * NZ
    mate = y * 2 + (1 - c)

    peers = [(blk, mate), (((x + 1) % NX) * NZ + z, uly), (((x + 3) % NX) * NZ + z, uly)]
    for step in range(1, NZ):
        for core in (0, 1):
            peers.append((line + (z + step) % NZ, y * 2 + core))
    greet(peers)

    def give(src, dst, send_sem, recv_sem, to_blk, to_uly, is_self):
        @pl.when(jnp.logical_not(is_self))
        def _():
            push(src, dst, send_sem, recv_sem, to_blk, to_uly).start()

        @pl.when(is_self)
        def _():
            pltpu.make_async_copy(src, dst, recv_sem).start()

    def given(src, dst, send_sem, recv_sem, to_blk, to_uly, is_self):
        @pl.when(jnp.logical_not(is_self))
        def _():
            push(src, dst, send_sem, recv_sem, to_blk, to_uly).wait_send()

    def kv_out(h, part):
        zd = 4 * c + h
        core = z % 2
        return (
            qkv_hbm.at[h, 1 + part], kv.at[blk, part], asem.at[h, 1 + part], kvsem.at[blk, part],
            line + zd, y * 2 + core, jnp.logical_and(zd == z, core == c),
        )

    def q_out(h):
        zd = 4 * c + h
        core = z // 4
        return (
            qkv_hbm.at[h, 0], qb.at[z % 4], asem.at[h, 0], qsem.at[z % 4],
            line + zd, y * 2 + core, jnp.logical_and(zd == z, core == c),
        )

    for h in range(3):
        for part in (0, 1):
            give(*kv_out(h, part))
    for h in range(3):
        give(*q_out(h))

    owner = z % 4 != 3

    def kv_arrive(slot, part):
        push(
            kv.at[slot, part], kv.at[slot, part], hsem.at[0], kvsem.at[slot, part], blk, mate
        ).wait_recv()

    def kv_send(slot, part, index, to_blk, to_uly):
        push(
            kv.at[slot, part], kv.at[slot, part], hsem.at[index], kvsem.at[slot, part],
            to_blk, to_uly,
        ).start()

    def o_out(i):
        core = z // 4
        h = z % 4
        to_z = 4 * c + i
        return (
            ob.at[i], back.at[h], osem.at[i], bsem.at[h],
            line + to_z, y * 2 + core, jnp.logical_and(to_z == z, core == c),
        )

    @pl.when(owner)
    def _():
        x_up = ((x + 1) % NX) * NZ + z
        x_dn = ((x + 3) % NX) * NZ + z
        odd = (z + c) % 2
        mine = []
        for near, far in ((0, 1), (2, 7), (6, 3), (4, 5)):
            mine.append((z + near + odd * (far - near)) % NZ)
        count = 0
        for zs in mine:
            slot = line + zs
            kv_arrive(slot, 0)
            kv_send(slot, 0, count, x_up, uly)
            kv_arrive(slot, 1)
            kv_send(slot, 1, count + 1, x_dn, uly)
            kv_send(slot, 1, count + 2, x_up, uly)
            kv_send(slot, 0, count + 3, x_dn, uly)
            kv_send(slot, 0, count + 4, blk, mate)
            kv_send(slot, 1, count + 5, blk, mate)
            count += 6
        for zs in mine:
            below = ((x + 3) % NX) * NZ + zs
            above = ((x + 1) % NX) * NZ + zs
            kv_arrive(below, 0)
            kv_send(below, 0, count, x_up, uly)
            kv_send(below, 0, count + 1, blk, mate)
            kv_arrive(above, 1)
            kv_send(above, 1, count + 2, x_dn, uly)
            kv_send(above, 1, count + 3, blk, mate)
            kv_arrive(below, 1)
            kv_send(below, 1, count + 4, blk, mate)
            kv_arrive(above, 0)
            kv_send(above, 0, count + 5, blk, mate)
            count += 6
        for zs in mine:
            across = ((x + 2) % NX) * NZ + zs
            for part in (0, 1):
                kv_arrive(across, part)
                kv_send(across, part, count + part, blk, mate)
            count += 2
        for zs in mine:
            other = zs + 1 - 2 * (zs % 2)
            for step in range(NX):
                for part in (0, 1):
                    kv_arrive(((x + step) % NX) * NZ + other, part)
        for i in range(4):
            push(qb.at[i], qb.at[i], hsem.at[0], qsem.at[i], blk, mate).wait_recv()

        factor = 1.0 / (HD**0.5)

        def one_tile(i, _):
            position = line + 4 * c + i
            row0 = corner_ref[position * 2]
            col0 = corner_ref[position * 2 + 1]
            queries = qb[i]
            slots = []
            best = None
            for w in range(WIN * WIN):
                slot = map_ref[(row0 + w // WIN) * GW + col0 + w % WIN]
                slots.append(slot)
                s = lax.dot_general(
                    queries, kv[slot, 0], (((1,), (1,)), ((), ())),
                    preferred_element_type=jnp.float32,
                )
                scores[w] = s
                for n in range(TILE // HD):
                    part = s[:, n * HD : (n + 1) * HD]
                    best = part if best is None else jnp.maximum(best, part)
            highest = jnp.max(best, axis=-1, keepdims=True)
            total = jnp.zeros((TILE, HD), jnp.float32)
            accum = jnp.zeros((TILE, HD), jnp.float32)
            for w in range(WIN * WIN):
                probs = jnp.exp((scores[w] - highest) * factor)
                for n in range(TILE // HD):
                    total = total + probs[:, n * HD : (n + 1) * HD]
                accum = accum + jnp.dot(
                    probs.astype(jnp.bfloat16), kv[slots[w], 1],
                    preferred_element_type=jnp.float32,
                )
            denom = jnp.sum(total, axis=-1, keepdims=True)
            ob[i] = (accum / denom).astype(ob.dtype)
            give(*o_out(i))
            return 0

        lax.fori_loop(0, 4, one_tile, 0)

        for index in range(count):
            push(
                kv.at[0, 0], kv.at[0, 0], hsem.at[index], kvsem.at[0, 0], blk, mate
            ).wait_send()
        for i in range(4):
            given(*o_out(i))

    for h in range(3):
        push(back.at[h], back.at[h], hsem.at[0], bsem.at[h], blk, mate).wait_recv()
        attn_ref[h] = back[h]
    for h in range(3):
        for part in (0, 1):
            given(*kv_out(h, part))
        given(*q_out(h))


def output_kernel(
    attn_ref, w_ref, gate_ref, out_ref,
    lhs, acc, give_mate, from_mate, relay_out, relay_in, fin_out, fin_in,
    msem, mrsem, ssem, rsem,
):
    blk, uly = where_am_i()
    y, c = uly // 2, uly % 2
    rows = out_ref.shape[0]
    width = out_ref.shape[1]
    half = width // 2
    up = ((y + 1) % NY) * 2 + c
    dn = ((y + 3) % NY) * 2 + c
    mate = y * 2 + (1 - c)
    greet([(blk, up), (blk, dn), (blk, mate)])

    order = (2, 1, 3, 0)
    for which, core in ((0, 1 - c), (1, c)):
        for n, step in enumerate(order):
            u = ((y + step) % NY) * 2 + core
            for h in range(3):
                lhs[which, pl.ds(n * rows, rows), pl.ds(h * HD, HD)] = attn_ref[
                    h, pl.ds(pl.multiple_of(u * rows, 16), rows), :
                ]

    part = jnp.dot(lhs[0], w_ref[...], preferred_element_type=jnp.float32)
    give_mate[...] = part.astype(give_mate.dtype).reshape(give_mate.shape)
    mates = []
    for n in range(4):
        copy = push(give_mate.at[n], from_mate.at[n], msem.at[n], mrsem.at[n], blk, mate)
        copy.start()
        mates.append(copy)
    acc[...] = jnp.dot(lhs[1], w_ref[...], preferred_element_type=jnp.float32).reshape(acc.shape)

    def cols(k):
        return slice(k * half, (k + 1) * half)

    def mixed(n, k):
        return acc[n, :, cols(k)] + from_mate[n, :, cols(k)].astype(jnp.float32)

    mates[0].wait_recv()
    sent = []
    for k, to in ((0, up), (1, dn)):
        relay_out[k] = mixed(0, k).astype(relay_out.dtype)
        copy = push(relay_out.at[k], relay_in.at[k], ssem.at[k], rsem.at[k], blk, to)
        copy.start()
        sent.append(copy)
    mates[1].wait_recv()
    mates[2].wait_recv()
    for d, to in ((0, up), (1, dn)):
        k = 1 - d
        fin_out[d, k] = mixed(1 + d, k).astype(fin_out.dtype)
        copy = push(
            fin_out.at[d, k], fin_in.at[d, k], ssem.at[2 + d * 2 + k], rsem.at[2 + d * 2 + k], blk, to
        )
        copy.start()
        sent.append(copy)
    for d, to in ((0, up), (1, dn)):
        k = d
        sent[k].wait_recv()
        fin_out[d, k] = (mixed(1 + d, k) + relay_in[k].astype(jnp.float32)).astype(fin_out.dtype)
        copy = push(
            fin_out.at[d, k], fin_in.at[d, k], ssem.at[2 + d * 2 + k], rsem.at[2 + d * 2 + k], blk, to
        )
        copy.start()
        sent.append(copy)
    mates[3].wait_recv()
    for copy in sent[2:]:
        copy.wait_recv()
    for k in (0, 1):
        total = mixed(3, k) + fin_in[0, k].astype(jnp.float32) + fin_in[1, k].astype(jnp.float32)
        out_ref[:, cols(k)] = (gate_ref[:, cols(k)] * total).astype(out_ref.dtype)
    for copy in sent + mates:
        copy.wait_send()


def vmem():
    return pl.BlockSpec(memory_space=pltpu.VMEM)


def hbm():
    return pl.BlockSpec(memory_space=pl.ANY)


def smem():
    return pl.BlockSpec(memory_space=pltpu.SMEM)


def params(collective_id):
    return pltpu.CompilerParams(
        collective_id=collective_id, has_side_effects=True, vmem_limit_bytes=VMEM_LIMIT
    )


def on_device(tokens, mod_shift, mod_scale, out_gate, w_qkv, w_out, tile_map, window_corner):
    rows, width = tokens.shape
    heads = w_qkv.shape[1]
    bf16 = jnp.bfloat16
    dma = pltpu.SemaphoreType.DMA
    qkv = pl.pallas_call(
        project_kernel,
        out_shape=jax.ShapeDtypeStruct((heads, 3, TILE, HD), bf16),
        in_specs=[vmem(), vmem(), vmem(), hbm()],
        out_specs=vmem(),
        scratch_shapes=[
            pltpu.VMEM((TILE, width), bf16),
            pltpu.VMEM((heads, width, 3 * HD), bf16),
            dma((3,)),
            dma((14,)),
            dma((8, 2)),
        ],
        compiler_params=params(0),
        name="project",
    )(tokens, mod_shift[None, :], mod_scale[None, :], jnp.transpose(w_qkv, (1, 0, 2)))

    attn = pl.pallas_call(
        attend_kernel,
        out_shape=jax.ShapeDtypeStruct((heads, TILE, HD), bf16),
        in_specs=[smem(), smem(), hbm()],
        out_specs=vmem(),
        scratch_shapes=[
            pltpu.VMEM((NX * NZ, 2, TILE, HD), bf16),
            pltpu.VMEM((4, TILE, HD), bf16),
            pltpu.VMEM((4, TILE, HD), bf16),
            pltpu.VMEM((3, TILE, HD), bf16),
            pltpu.VMEM((WIN * WIN, TILE, TILE), jnp.float32),
            dma((3, 3)),
            dma((4,)),
            dma((NX * NZ, 2)),
            dma((3,)),
            dma((56,)),
            dma((4,)),
        ],
        compiler_params=params(1),
        name="attend",
    )(tile_map, window_corner.reshape(-1), qkv)

    return pl.pallas_call(
        output_kernel,
        out_shape=jax.ShapeDtypeStruct((rows, width), bf16),
        in_specs=[vmem(), vmem(), vmem()],
        out_specs=vmem(),
        scratch_shapes=[
            pltpu.VMEM((2, 4 * rows, heads * HD), bf16),
            pltpu.VMEM((4, rows, width), jnp.float32),
            pltpu.VMEM((4, rows, width), bf16),
            pltpu.VMEM((4, rows, width), bf16),
            pltpu.VMEM((2, rows, width // 2), bf16),
            pltpu.VMEM((2, rows, width // 2), bf16),
            pltpu.VMEM((2, 2, rows, width // 2), bf16),
            pltpu.VMEM((2, 2, rows, width // 2), bf16),
            dma((4,)),
            dma((4,)),
            dma((6,)),
            dma((6,)),
        ],
        compiler_params=params(2),
        name="output",
    )(attn, w_out, out_gate[None, :])


def solution(mesh):
    in_specs = (
        P(("blk", "uly"), None),
        P(),
        P(),
        P(),
        P(None, "uly", None),
        P("uly", None),
        P(),
        P(),
    )
    out_specs = P(("blk", "uly"), None)
    return jax.shard_map(
        on_device, mesh=mesh, in_specs=in_specs, out_specs=out_specs, check_vma=False
    )
```

time: 697 us -> 105 us (0.15)
  the two profiles are of different devices: /device:TPU:1 before, /device:TPU:96 now
where the time goes in v1:
time: 105 us
  Pallas kernels  102 us (97%)
  local copies, waits for them, and re-layouts  3.07 us (3%)
    pallas_call x1, Pallas kernels, on_device(): pl.pallas_call(attend_kernel, out_shape=jax.ShapeDtypeStruct((heads, TILE...  62.4 us
    pallas_call x1, Pallas kernels, on_device(): pl.pallas_call(project_kernel, out_shape=jax.ShapeDtypeStruct((heads, 3,...  20.8 us
    pallas_call x1, Pallas kernels, on_device(): pl.pallas_call(output_kernel, out_shape=jax.ShapeDtypeStruct((rows, width...  18.8 us
    unnamed x2, local copies, waits for them, and re-layouts  2.45 us

profile of v1, /device:TPU:96, one launch (start us, length us, event | category | flops | bytes accessed | tf_op | source)
XLA Modules:
  0.0 105.1 jit_solution(12978903433933101456)
XLA Ops:
  0.0 0.8 copy.10
  0.8 0.6 reshape.3.corner_ref
  1.4 20.8 %project.1.qkv_hbm = bf16[3,3,384,128]{3,2,1,0:T(8,128)(2,1)} custom-call(bf16[48,3072]{1,0:T(8,128)(2,1)} %x_ref.1, f32[1,3072]{1,0:T(1,128)} %bitcast.5, f32[1,3072]{1,0:T(1,128)} %bitcast.6, bf16[3,3072,384]{2,1,0:T(8,128)(2,1)} %bitcast.4), custom_call_target="tpu_custom_call" | custom-call | tf_op jit(solution)/shard_map/project/pallas_call | solution.py:386
  22.2 62.4 %attend.1.attn_ref = bf16[3,384,128]{2,1,0:T(8,128)(2,1)} custom-call(s32[32]{0:T(128)} %map_ref.1, s32[64]{0:T(128)} %reshape.3.corner_ref, bf16[3,3,384,128]{3,2,1,0:T(8,128)(2,1)} %project.1.qkv_hbm), custom_call_target="tpu_custom_call" | custom-call | tf_op jit(solution)/shard_map/attend/pallas_call | solution.py:402
  84.6 18.8 %output.1 = bf16[48,3072]{1,0:T(8,128)(2,1)} custom-call(bf16[3,384,128]{2,1,0:T(8,128)(2,1)} %attend.1.attn_ref, bf16[384,3072]{1,0:T(8,128)(2,1)} %w_ref.1, f32[1,3072]{1,0:T(1,128)} %bitcast.7), custom_call_target="tpu_custom_call" | custom-call | tf_op jit(solution)/shard_map/output/pallas_call | solution.py:424
  103.4 1.7 %copy.12 = bf16[48,3072]{1,0:T(8,128)(2,1)} copy(bf16[48,3072]{1,0:T(8,128)(2,1)} %output.1) | data formatting | bytes 589824

commit v2 on v1

v2 whole, which is shorter than its diff:
```python
import jax
import jax.numpy as jnp
from jax import lax
from jax.experimental import pallas as pl
from jax.experimental.pallas import tpu as pltpu
from jax.sharding import PartitionSpec as P

TILE = 384
WIN = 3
GW = 4
NX = 4
NZ = 8
NY = 4
HD = 128
MESH = pl.DeviceIdType.MESH
VMEM_LIMIT = 62 * 1024 * 1024


def push(src, dst, send_sem, recv_sem, blk, uly):
    return pltpu.make_async_remote_copy(
        src_ref=src,
        dst_ref=dst,
        send_sem=send_sem,
        recv_sem=recv_sem,
        device_id={"blk": blk, "uly": uly},
        device_id_type=MESH,
    )


def block_kernel(
    map_ref, corner_ref, x_ref, shift_ref, scale_ref, gate_ref, w_hbm, wo_hbm, out_ref,
    xbuf, wkv, wq, wo, stage, kv, qb, ob, back, scores,
    lhs, acc, give_mate, from_mate, relay_out, relay_in, fin_out, fin_in,
    wsem, wosem, gsem, grsem, asem, aqsem, kvsem, acrsem, matesem, fsem, qsem, bsem, osem,
    msem, mrsem, ssem, rsem,
):
    blk = lax.axis_index("blk")
    uly = lax.axis_index("uly")
    y, c = uly // 2, uly % 2
    x, z = blk // NZ, blk % NZ
    line = x * NZ
    rows, width = x_ref.shape
    half = width // 2
    chunk = 2 * rows
    heads = w_hbm.shape[0]
    up = ((y + 1) % NY) * 2 + c
    dn = ((y + 3) % NY) * 2 + c
    opp = ((y + 2) % NY) * 2 + c
    mate = y * 2 + (1 - c)
    x_up = ((x + 1) % NX) * NZ + z
    x_dn = ((x + 3) % NX) * NZ + z
    owner = z % 4 != 3

    weights = []
    for h in range(heads):
        weights.append(
            pltpu.make_async_copy(w_hbm.at[h, :, pl.ds(HD, 2 * HD)], wkv.at[h], wsem.at[h])
        )
    for h in range(heads):
        weights.append(
            pltpu.make_async_copy(
                w_hbm.at[h, :, pl.ds(0, HD)], wq.at[:, pl.ds(h * HD, HD)], wsem.at[heads + h]
            )
        )
    weights.append(pltpu.make_async_copy(wo_hbm, wo, wosem))
    for copy in weights:
        copy.start()

    peers = [(blk, mate), (blk, up), (blk, dn), (x_up, uly), (x_dn, uly)]
    for step in range(1, NZ):
        for core in (0, 1):
            peers.append((line + (z + step) % NZ, y * 2 + core))
    barrier = pltpu.get_barrier_semaphore()
    for to_blk, to_uly in peers:
        pl.semaphore_signal(
            barrier, inc=1, device_id={"blk": to_blk, "uly": to_uly}, device_id_type=MESH
        )

    values = x_ref[...].astype(jnp.float32)
    mean = jnp.mean(values, axis=-1, keepdims=True)
    centred = values - mean
    var = jnp.mean(centred * centred, axis=-1, keepdims=True)
    normed = centred * lax.rsqrt(var + 1e-06) * (1.0 + scale_ref[...]) + shift_ref[...]
    xbuf[pl.ds(pl.multiple_of(uly * rows, 16), rows), :] = normed.astype(xbuf.dtype)

    pl.semaphore_wait(barrier, len(peers))

    def piece(u, k):
        return xbuf.at[pl.ds(pl.multiple_of(u * rows, 16), rows), pl.ds(k * half, half)]

    gathered = []

    def spread(u, k, to):
        copy = push(piece(u, k), piece(u, k), gsem.at[len(gathered)], grsem.at[u, k], blk, to)
        copy.start()
        gathered.append(copy)

    def arrive(u, k):
        push(piece(u, k), piece(u, k), gsem.at[0], grsem.at[u, k], blk, mate).wait_recv()

    def chunk_rows(step):
        return pl.ds(pl.multiple_of(((y + step) % NY) * chunk, 16), chunk)

    def give(src, dst, send_sem, recv_sem, to_blk, to_uly, is_self):
        @pl.when(jnp.logical_not(is_self))
        def _():
            push(src, dst, send_sem, recv_sem, to_blk, to_uly).start()

        @pl.when(is_self)
        def _():
            pltpu.make_async_copy(src, dst, recv_sem).start()

    def given(src, dst, send_sem, recv_sem, to_blk, to_uly, is_self):
        @pl.when(jnp.logical_not(is_self))
        def _():
            push(src, dst, send_sem, recv_sem, to_blk, to_uly).wait_send()

    def turn(n):
        return (z + n) % heads

    def kv_out(n, step):
        h = turn(n)
        zd = 4 * c + h
        core = z % 2
        at = chunk_rows(step)
        return (
            stage.at[h, pl.ds(1, 2), at], kv.at[blk, :, at], asem.at[n, step],
            kvsem.at[blk, (y + step) % NY],
            line + zd, y * 2 + core, jnp.logical_and(zd == z, core == c),
        )

    def q_out(n):
        h = turn(n)
        zd = 4 * c + h
        core = z // 4
        return (
            stage.at[h, 0], qb.at[z % 4], aqsem.at[n], qsem.at[z % 4],
            line + zd, y * 2 + core, jnp.logical_and(zd == z, core == c),
        )

    def project(steps):
        left = jnp.concatenate([xbuf[chunk_rows(step), :] for step in steps], axis=0)
        for h in range(heads):
            result = jnp.dot(left, wkv[h], preferred_element_type=jnp.float32)
            for n, step in enumerate(steps):
                for part in (0, 1):
                    stage[h, 1 + part, chunk_rows(step), :] = result[
                        n * chunk : (n + 1) * chunk, part * HD : (part + 1) * HD
                    ].astype(stage.dtype)
        for step in steps:
            for n in range(heads):
                give(*kv_out(n, step))

    odd = (z + c) % 2
    mine = []
    for even_gap, odd_gap in ((0, 1), (2, 7), (6, 3), (4, 5)):
        mine.append((z + even_gap + odd * (odd_gap - even_gap)) % NZ)
    X_UP, X_DN, MATE_LINE, MATE_BELOW, MATE_ABOVE, RELAY_UP, RELAY_DN, MATE_ACROSS = range(8)

    def kv_part(slot, step, part):
        at = chunk_rows(step)
        if part is None:
            return kv.at[slot, :, at]
        return kv.at[slot, part, at]

    def kv_wait(slot, step):
        ref = kv_part(slot, step, None)
        push(ref, ref, fsem.at[0], kvsem.at[slot, (y + step) % NY], blk, mate).wait_recv()

    def kv_pass(slot, step, kind, to_blk, to_uly, recv_sem, part=None):
        ref = kv_part(slot, step, part)
        push(ref, ref, fsem.at[kind], recv_sem, to_blk, to_uly).start()

    def pump_line(step):
        n = (y + step) % NY
        for zs in mine:
            slot = line + zs
            kv_wait(slot, step)
            kv_pass(slot, step, X_UP, x_up, uly, kvsem.at[slot, n])
            kv_pass(slot, step, X_DN, x_dn, uly, kvsem.at[slot, n])
            kv_pass(slot, step, MATE_LINE, blk, mate, matesem)

    def pump_sides(step):
        n = (y + step) % NY
        for zs in mine:
            below = ((x + 3) % NX) * NZ + zs
            above = ((x + 1) % NX) * NZ + zs
            kv_wait(below, step)
            kv_pass(below, step, RELAY_UP, x_up, uly, acrsem.at[zs, n, 0], part=0)
            kv_pass(below, step, MATE_BELOW, blk, mate, matesem)
            kv_wait(above, step)
            kv_pass(above, step, RELAY_DN, x_dn, uly, acrsem.at[zs, n, 1], part=1)
            kv_pass(above, step, MATE_ABOVE, blk, mate, matesem)

    def pump_across(step):
        n = (y + step) % NY
        for zs in mine:
            across = ((x + 2) % NX) * NZ + zs
            for part in (0, 1):
                ref = kv_part(across, step, part)
                push(ref, ref, fsem.at[0], acrsem.at[zs, n, part], blk, mate).wait_recv()
                kv_pass(across, step, MATE_ACROSS, blk, mate, matesem, part=part)

    for first in (0, 1):
        spread(uly, first, up)
        spread(uly, 1 - first, dn)
        spread(uly, first, mate)
    for k in (0, 1):
        arrive(mate, k)
    for h in range(heads):
        weights[h].wait()
    project((0,))

    def mate_of(u):
        return u + 1 - 2 * c

    arrive(dn, 0)
    spread(dn, 0, up)
    spread(dn, 0, mate)
    arrive(up, 1)
    spread(up, 1, dn)
    spread(up, 1, mate)
    arrive(dn, 1)
    spread(dn, 1, mate)
    arrive(up, 0)
    spread(up, 0, mate)
    for k in (0, 1):
        arrive(mate_of(dn), k)
        arrive(mate_of(up), k)
    project((3, 1))

    @pl.when(owner)
    def _():
        pump_line(0)

    arrive(opp, 0)
    spread(opp, 0, mate)
    arrive(opp, 1)
    spread(opp, 1, mate)
    for k in (0, 1):
        arrive(mate_of(opp), k)
    project((2,))
    for h in range(heads):
        weights[heads + h].wait()
    result = jnp.dot(xbuf[...], wq[...], preferred_element_type=jnp.float32)
    for h in range(heads):
        stage[h, 0] = result[:, h * HD : (h + 1) * HD].astype(stage.dtype)
    for n in range(heads):
        give(*q_out(n))

    def o_out(i):
        core = z // 4
        h = z % 4
        to_z = 4 * c + i
        return (
            ob.at[i], back.at[h], osem.at[i], bsem.at[h],
            line + to_z, y * 2 + core, jnp.logical_and(to_z == z, core == c),
        )

    @pl.when(owner)
    def _():
        pump_line(3)
        pump_line(1)
        pump_sides(0)
        pump_line(2)
        pump_sides(3)
        pump_sides(1)
        pump_across(0)
        pump_sides(2)
        pump_across(3)
        pump_across(1)
        pump_across(2)
        sixteen = kv.at[pl.ds(0, 16)]
        push(sixteen, sixteen, fsem.at[0], matesem, blk, mate).wait_recv()
        for i in range(4):
            push(qb.at[i], qb.at[i], fsem.at[0], qsem.at[i], blk, mate).wait_recv()

        factor = 1.0 / (HD**0.5)

        def one_tile(n, _):
            i = (n + z) % 4
            position = line + 4 * c + i
            row0 = corner_ref[0, position]
            col0 = corner_ref[1, position]
            queries = qb[i]
            slots = []
            best = None
            for w in range(WIN * WIN):
                slot = map_ref[(row0 + w // WIN) * GW + col0 + w % WIN]
                slots.append(slot)
                s = lax.dot_general(
                    queries, kv[slot, 0], (((1,), (1,)), ((), ())),
                    preferred_element_type=jnp.float32,
                )
                scores[w] = s
                for n3 in range(TILE // HD):
                    part = s[:, n3 * HD : (n3 + 1) * HD]
                    best = part if best is None else jnp.maximum(best, part)
            highest = jnp.max(best, axis=-1, keepdims=True)
            total = jnp.zeros((TILE, HD), jnp.float32)
            accum = jnp.zeros((TILE, HD), jnp.float32)
            for w in range(WIN * WIN):
                probs = jnp.exp((scores[w] - highest) * factor)
                for n3 in range(TILE // HD):
                    total = total + probs[:, n3 * HD : (n3 + 1) * HD]
                accum = accum + jnp.dot(
                    probs.astype(jnp.bfloat16), kv[slots[w], 1],
                    preferred_element_type=jnp.float32,
                )
            denom = jnp.sum(total, axis=-1, keepdims=True)
            ob[i] = (accum / denom).astype(ob.dtype)
            give(*o_out(i))
            return 0

        lax.fori_loop(0, 4, one_tile, 0)

    weights[-1].wait()
    for h in range(heads):
        push(back.at[h], back.at[h], fsem.at[0], bsem.at[h], blk, mate).wait_recv()
    order = (2, 1, 3, 0)
    for which, core in ((0, 1 - c), (1, c)):
        for n, step in enumerate(order):
            u = ((y + step) % NY) * 2 + core
            for h in range(heads):
                lhs[which, pl.ds(n * rows, rows), pl.ds(h * HD, HD)] = back[
                    h, pl.ds(pl.multiple_of(u * rows, 16), rows), :
                ]

    part = jnp.dot(lhs[0], wo[...], preferred_element_type=jnp.float32)
    give_mate[...] = part.astype(give_mate.dtype).reshape(give_mate.shape)
    mates = []
    for n in range(4):
        copy = push(give_mate.at[n], from_mate.at[n], msem.at[n], mrsem.at[n], blk, mate)
        copy.start()
        mates.append(copy)
    acc[...] = jnp.dot(lhs[1], wo[...], preferred_element_type=jnp.float32).reshape(acc.shape)

    def cols(k):
        return slice(k * half, (k + 1) * half)

    def mixed(n, k):
        return acc[n, :, cols(k)] + from_mate[n, :, cols(k)].astype(jnp.float32)

    mates[0].wait_recv()
    sent = []
    for k, to in ((0, up), (1, dn)):
        relay_out[k] = mixed(0, k).astype(relay_out.dtype)
        copy = push(relay_out.at[k], relay_in.at[k], ssem.at[k], rsem.at[k], blk, to)
        copy.start()
        sent.append(copy)
    mates[1].wait_recv()
    mates[2].wait_recv()

    def finish(d, k, to, extra):
        value = mixed(1 + d, k)
        if extra is not None:
            value = value + extra
        fin_out[d, k] = value.astype(fin_out.dtype)
        n = 2 + d * 2 + k
        copy = push(fin_out.at[d, k], fin_in.at[d, k], ssem.at[n], rsem.at[n], blk, to)
        copy.start()
        sent.append(copy)

    for d, to in ((0, up), (1, dn)):
        finish(d, 1 - d, to, None)
    for d, to in ((0, up), (1, dn)):
        sent[d].wait_recv()
        finish(d, d, to, relay_in[d].astype(jnp.float32))
    mates[3].wait_recv()
    for copy in sent[2:]:
        copy.wait_recv()
    for k in (0, 1):
        total = mixed(3, k) + fin_in[0, k].astype(jnp.float32) + fin_in[1, k].astype(jnp.float32)
        out_ref[:, cols(k)] = (gate_ref[:, cols(k)] * total).astype(out_ref.dtype)

    for copy in gathered + sent + mates:
        copy.wait_send()
    for n in range(heads):
        for step in range(NY):
            given(*kv_out(n, step))
        given(*q_out(n))

    @pl.when(owner)
    def _():
        for kind in range(8):
            tiles = 2 if kind in (RELAY_UP, RELAY_DN) else 4
            ref = kv.at[pl.ds(0, tiles)]
            push(ref, ref, fsem.at[kind], matesem, blk, mate).wait_send()
        for i in range(4):
            given(*o_out(i))


def vmem():
    return pl.BlockSpec(memory_space=pltpu.VMEM)


def hbm():
    return pl.BlockSpec(memory_space=pl.ANY)


def smem():
    return pl.BlockSpec(memory_space=pltpu.SMEM)


def on_device(tokens, mod_shift, mod_scale, out_gate, w_qkv, w_out, tile_map, window_corner):
    rows, width = tokens.shape
    heads = w_qkv.shape[1]
    bf16 = jnp.bfloat16
    f32 = jnp.float32
    dma = pltpu.SemaphoreType.DMA
    return pl.pallas_call(
        block_kernel,
        out_shape=jax.ShapeDtypeStruct((rows, width), bf16),
        in_specs=[smem(), smem(), vmem(), vmem(), vmem(), vmem(), hbm(), hbm()],
        out_specs=vmem(),
        scratch_shapes=[
            pltpu.VMEM((TILE, width), bf16),
            pltpu.VMEM((heads, width, 2 * HD), bf16),
            pltpu.VMEM((width, heads * HD), bf16),
            pltpu.VMEM((heads * HD, width), bf16),
            pltpu.VMEM((heads, 3, TILE, HD), bf16),
            pltpu.VMEM((NX * NZ, 2, TILE, HD), bf16),
            pltpu.VMEM((4, TILE, HD), bf16),
            pltpu.VMEM((4, TILE, HD), bf16),
            pltpu.VMEM((heads, TILE, HD), bf16),
            pltpu.VMEM((WIN * WIN, TILE, TILE), f32),
            pltpu.VMEM((2, 4 * rows, heads * HD), bf16),
            pltpu.VMEM((4, rows, width), f32),
            pltpu.VMEM((4, rows, width), bf16),
            pltpu.VMEM((4, rows, width), bf16),
            pltpu.VMEM((2, rows, width // 2), bf16),
            pltpu.VMEM((2, rows, width // 2), bf16),
            pltpu.VMEM((2, 2, rows, width // 2), bf16),
            pltpu.VMEM((2, 2, rows, width // 2), bf16),
            dma((6,)),
            dma,
            dma((14,)),
            dma((8, 2)),
            dma((3, 4)),
            dma((3,)),
            dma((NX * NZ, 4)),
            dma((NZ, 4, 2)),
            dma,
            dma((8,)),
            dma((4,)),
            dma((3,)),
            dma((4,)),
            dma((4,)),
            dma((4,)),
            dma((6,)),
            dma((6,)),
        ],
        compiler_params=pltpu.CompilerParams(
            collective_id=0, has_side_effects=True, vmem_limit_bytes=VMEM_LIMIT
        ),
        name="block",
    )(
        tile_map, window_corner.T, tokens, mod_shift[None, :], mod_scale[None, :],
        out_gate[None, :], jnp.transpose(w_qkv, (1, 0, 2)), w_out,
    )


def solution(mesh):
    in_specs = (
        P(("blk", "uly"), None),
        P(),
        P(),
        P(),
        P(None, "uly", None),
        P("uly", None),
        P(),
        P(),
    )
    out_specs = P(("blk", "uly"), None)
    return jax.shard_map(
        on_device, mesh=mesh, in_specs=in_specs, out_specs=out_specs, check_vma=False
    )
```

time: 105 us -> 86.4 us (0.82)
  the two profiles are of different devices: /device:TPU:96 before, /device:TPU:1 now
where the time goes in v2:
time: 86.4 us; the launch traced here: 86 us
  Pallas kernels  84.3 us (98%)
  local copies, waits for them, and re-layouts  1.69 us (2%)
    pallas_call x1, Pallas kernels, on_device(): pl.pallas_call(block_kernel, out_shape=jax.ShapeDtypeStruct((rows, width)...  84.3 us

profile of v2, /device:TPU:1, one launch (start us, length us, event | category | flops | bytes accessed | tf_op | source)
XLA Modules:
  0.0 86.0 jit_solution(13762316591962722233)
XLA Ops:
  0.0 84.3 %block.1 = bf16[48,3072]{1,0:T(8,128)(2,1)} custom-call(s32[32]{0:T(128)} %map_ref.1, s32[2,32]{1,0:T(2,128)} %bitcast.9, bf16[48,3072]{1,0:T(8,128)(2,1)} %x_ref.1, f32[1,3072]{1,0:T(1,128)} %bitcast.6, f32[1,3072]{1,0:T(1,128)} %bitcast.7, f32[1,3072]{1,0:T(1,128)} %bitcast.8, bf16[3,3072,384]{2,1,0:T(8,128)(2,1)} %bitcast.5, bf16[384,3072]{1,0:T(8,128)(2,1)} %wo_hbm.1), custom_call_target="tpu_custom_call" | custom-call | tf_op jit(solution)/shard_map/block/pallas_call | solution.py:411
  84.3 1.7 %copy.10 = bf16[48,3072]{1,0:T(8,128)(2,1)} copy(bf16[48,3072]{1,0:T(8,128)(2,1)} %block.1) | data formatting | bytes 589824

commit v3 on v2

--- a/solution.py
+++ b/solution.py
@@ -29,10 +29,10 @@
 
 def block_kernel(
     map_ref, corner_ref, x_ref, shift_ref, scale_ref, gate_ref, w_hbm, wo_hbm, out_ref,
-    xbuf, wkv, wq, wo, stage, kv, qb, ob, back, scores,
+    xbuf, wkv, wq, wo, stage, kv, qb, ob_first, ob_last, edge_out, back, scores,
     lhs, acc, give_mate, from_mate, relay_out, relay_in, fin_out, fin_in,
-    wsem, wosem, gsem, grsem, asem, aqsem, kvsem, acrsem, matesem, fsem, qsem, bsem, osem,
-    msem, mrsem, ssem, rsem,
+    wsem, wosem, gsem, grsem, asem, aqsem, kvsem, matesem, fsem, qsem, bsem, osem,
+    qxsem, qxrsem, oxsem, oxrsem, msem, mrsem, ssem, rsem,
 ):
     blk = lax.axis_index("blk")
     uly = lax.axis_index("uly")
@@ -50,6 +50,8 @@
     x_up = ((x + 1) % NX) * NZ + z
     x_dn = ((x + 3) % NX) * NZ + z
     owner = z % 4 != 3
+    beyond = ((x + 3 + 2 * c) % NX) * NZ + z
+    edge = 3 * c
 
     weights = []
     for h in range(heads):
@@ -66,7 +68,7 @@
     for copy in weights:
         copy.start()
 
-    peers = [(blk, mate), (blk, up), (blk, dn), (x_up, uly), (x_dn, uly)]
+    peers = [(blk, mate), (blk, up), (blk, dn), (x_up, uly), (x_dn, uly), (beyond, mate)]
     for step in range(1, NZ):
         for core in (0, 1):
             peers.append((line + (z + step) % NZ, y * 2 + core))
@@ -129,14 +131,27 @@
             line + zd, y * 2 + core, jnp.logical_and(zd == z, core == c),
         )
 
-    def q_out(n):
+    def q_out(n, step):
         h = turn(n)
         zd = 4 * c + h
         core = z // 4
+        at = chunk_rows(step)
         return (
-            stage.at[h, 0], qb.at[z % 4], aqsem.at[n], qsem.at[z % 4],
+            stage.at[h, 0, at], qb.at[z % 4, at], aqsem.at[n, step], qsem.at[z % 4],
             line + zd, y * 2 + core, jnp.logical_and(zd == z, core == c),
         )
+
+    def project_queries(steps):
+        left = jnp.concatenate([xbuf[chunk_rows(step), :] for step in steps], axis=0)
+        result = jnp.dot(left, wq[...], preferred_element_type=jnp.float32)
+        for h in range(heads):
+            for n, step in enumerate(steps):
+                stage[h, 0, chunk_rows(step), :] = result[
+                    n * chunk : (n + 1) * chunk, h * HD : (h + 1) * HD
+                ].astype(stage.dtype)
+        for n in range(heads):
+            for step in steps:
+                give(*q_out(n, step))
 
     def project(steps):
         left = jnp.concatenate([xbuf[chunk_rows(step), :] for step in steps], axis=0)
@@ -155,20 +170,17 @@
     mine = []
     for even_gap, odd_gap in ((0, 1), (2, 7), (6, 3), (4, 5)):
         mine.append((z + even_gap + odd * (odd_gap - even_gap)) % NZ)
-    X_UP, X_DN, MATE_LINE, MATE_BELOW, MATE_ABOVE, RELAY_UP, RELAY_DN, MATE_ACROSS = range(8)
-
-    def kv_part(slot, step, part):
-        at = chunk_rows(step)
-        if part is None:
-            return kv.at[slot, :, at]
-        return kv.at[slot, part, at]
+    X_UP, X_DN, MATE_LINE, MATE_BELOW, MATE_ABOVE, RELAY, MATE_ACROSS = range(7)
+
+    def kv_part(slot, step):
+        return kv.at[slot, :, chunk_rows(step)]
 
     def kv_wait(slot, step):
-        ref = kv_part(slot, step, None)
+        ref = kv_part(slot, step)
         push(ref, ref, fsem.at[0], kvsem.at[slot, (y + step) % NY], blk, mate).wait_recv()
 
-    def kv_pass(slot, step, kind, to_blk, to_uly, recv_sem, part=None):
-        ref = kv_part(slot, step, part)
+    def kv_pass(slot, step, kind, to_blk, to_uly, recv_sem):
+        ref = kv_part(slot, step)
         push(ref, ref, fsem.at[kind], recv_sem, to_blk, to_uly).start()
 
     def pump_line(step):
@@ -186,20 +198,16 @@
             below = ((x + 3) % NX) * NZ + zs
             above = ((x + 1) % NX) * NZ + zs
             kv_wait(below, step)
-            kv_pass(below, step, RELAY_UP, x_up, uly, acrsem.at[zs, n, 0], part=0)
             kv_pass(below, step, MATE_BELOW, blk, mate, matesem)
             kv_wait(above, step)
-            kv_pass(above, step, RELAY_DN, x_dn, uly, acrsem.at[zs, n, 1], part=1)
             kv_pass(above, step, MATE_ABOVE, blk, mate, matesem)
+        far = ((x + 1 + 2 * c) % NX) * NZ + 7 * c
+        kv_pass(far, step, RELAY, beyond, uly, kvsem.at[far, n])
 
     def pump_across(step):
-        n = (y + step) % NY
-        for zs in mine:
-            across = ((x + 2) % NX) * NZ + zs
-            for part in (0, 1):
-                ref = kv_part(across, step, part)
-                push(ref, ref, fsem.at[0], acrsem.at[zs, n, part], blk, mate).wait_recv()
-                kv_pass(across, step, MATE_ACROSS, blk, mate, matesem, part=part)
+        across = ((x + 2) % NX) * NZ + 7 * c
+        kv_wait(across, step)
+        kv_pass(across, step, MATE_ACROSS, blk, mate, matesem)
 
     for first in (0, 1):
         spread(uly, first, up)
@@ -210,6 +218,9 @@
     for h in range(heads):
         weights[h].wait()
     project((0,))
+    for h in range(heads):
+        weights[heads + h].wait()
+    project_queries((0,))
 
     def mate_of(u):
         return u + 1 - 2 * c
@@ -240,22 +251,28 @@
     for k in (0, 1):
         arrive(mate_of(opp), k)
     project((2,))
-    for h in range(heads):
-        weights[heads + h].wait()
-    result = jnp.dot(xbuf[...], wq[...], preferred_element_type=jnp.float32)
-    for h in range(heads):
-        stage[h, 0] = result[:, h * HD : (h + 1) * HD].astype(stage.dtype)
-    for n in range(heads):
-        give(*q_out(n))
-
-    def o_out(i):
+    project_queries((3, 1, 2))
+
+    order = (2, 1, 3, 0)
+    obs = (ob_first, ob_last)
+
+    def o_out(which, i, n, src):
         core = z // 4
         h = z % 4
         to_z = 4 * c + i
+        step = order[2 * which + n]
         return (
-            ob.at[i], back.at[h], osem.at[i], bsem.at[h],
+            src.at[pl.ds(n * chunk, chunk)], back.at[h, chunk_rows(step)],
+            osem.at[which, i, n], bsem.at[h, (y + step) % NY],
             line + to_z, y * 2 + core, jnp.logical_and(to_z == z, core == c),
         )
+
+    def q_trade():
+        return push(qb.at[edge], qb.at[4], qxsem, qxrsem, beyond, mate)
+
+    def o_trade(which):
+        ob = obs[which]
+        return push(ob.at[edge], ob.at[4], oxsem.at[which], oxrsem.at[which], beyond, mate)
 
     @pl.when(owner)
     def _():
@@ -266,74 +283,101 @@
         pump_sides(3)
         pump_sides(1)
         pump_across(0)
+        for i in range(4):
+            push(qb.at[i], qb.at[i], fsem.at[0], qsem.at[i], blk, mate).wait_recv()
+        q_trade().start()
         pump_sides(2)
         pump_across(3)
         pump_across(1)
         pump_across(2)
-        sixteen = kv.at[pl.ds(0, 16)]
-        push(sixteen, sixteen, fsem.at[0], matesem, blk, mate).wait_recv()
-        for i in range(4):
-            push(qb.at[i], qb.at[i], fsem.at[0], qsem.at[i], blk, mate).wait_recv()
+        rest = kv.at[pl.ds(0, 13)]
+        push(rest, rest, fsem.at[0], matesem, blk, mate).wait_recv()
+        q_trade().wait_recv()
 
         factor = 1.0 / (HD**0.5)
-
-        def one_tile(n, _):
-            i = (n + z) % 4
-            position = line + 4 * c + i
-            row0 = corner_ref[0, position]
-            col0 = corner_ref[1, position]
-            queries = qb[i]
-            slots = []
-            best = None
-            for w in range(WIN * WIN):
-                slot = map_ref[(row0 + w // WIN) * GW + col0 + w % WIN]
-                slots.append(slot)
-                s = lax.dot_general(
-                    queries, kv[slot, 0], (((1,), (1,)), ((), ())),
-                    preferred_element_type=jnp.float32,
-                )
-                scores[w] = s
-                for n3 in range(TILE // HD):
-                    part = s[:, n3 * HD : (n3 + 1) * HD]
-                    best = part if best is None else jnp.maximum(best, part)
-            highest = jnp.max(best, axis=-1, keepdims=True)
-            total = jnp.zeros((TILE, HD), jnp.float32)
-            accum = jnp.zeros((TILE, HD), jnp.float32)
-            for w in range(WIN * WIN):
-                probs = jnp.exp((scores[w] - highest) * factor)
-                for n3 in range(TILE // HD):
-                    total = total + probs[:, n3 * HD : (n3 + 1) * HD]
-                accum = accum + jnp.dot(
-                    probs.astype(jnp.bfloat16), kv[slots[w], 1],
-                    preferred_element_type=jnp.float32,
-                )
-            denom = jnp.sum(total, axis=-1, keepdims=True)
-            ob[i] = (accum / denom).astype(ob.dtype)
-            give(*o_out(i))
-            return 0
-
-        lax.fori_loop(0, 4, one_tile, 0)
+        end = line + 4 * c + edge
+        swapped = jnp.clip((map_ref[end] - end) * (2 * c - 1), 0, 1)
+
+        def attend(which):
+            ob = obs[which]
+            spans = [chunk_rows(step) for step in order[2 * which : 2 * which + 2]]
+
+            def one_tile(n, _):
+                inner = jnp.minimum(n, 1)
+                i = (edge + inner * (1 + (n + 2 + z) % 3)) % 4
+                other = (1 - inner) * swapped
+                position = line + 4 * c + i + other * (2 * c - 1)
+                row0 = corner_ref[0, position]
+                col0 = corner_ref[1, position]
+                at = i + other * (4 - i)
+                queries = jnp.concatenate([qb[at, span, :] for span in spans], axis=0)
+                slots = []
+                best = None
+                for w in range(WIN * WIN):
+                    slot = map_ref[(row0 + w // WIN) * GW + col0 + w % WIN]
+                    slots.append(slot)
+                    s = lax.dot_general(
+                        queries, kv[slot, 0], (((1,), (1,)), ((), ())),
+                        preferred_element_type=jnp.float32,
+                    )
+                    scores[w] = s
+                    for m in range(TILE // HD):
+                        part = s[:, m * HD : (m + 1) * HD]
+                        best = part if best is None else jnp.maximum(best, part)
+                highest = jnp.max(best, axis=-1, keepdims=True)
+                total = jnp.zeros((2 * chunk, HD), jnp.float32)
+                accum = jnp.zeros((2 * chunk, HD), jnp.float32)
+                for w in range(WIN * WIN):
+                    probs = jnp.exp((scores[w] - highest) * factor)
+                    for m in range(TILE // HD):
+                        total = total + probs[:, m * HD : (m + 1) * HD]
+                    accum = accum + jnp.dot(
+                        probs.astype(jnp.bfloat16), kv[slots[w], 1],
+                        preferred_element_type=jnp.float32,
+                    )
+                denom = jnp.sum(total, axis=-1, keepdims=True)
+                ob[i] = (accum / denom).astype(ob.dtype)
+
+                @pl.when(n == 0)
+                def _():
+                    o_trade(which).start()
+
+                @pl.when(n > 0)
+                def _():
+                    for m in (0, 1):
+                        give(*o_out(which, i, m, ob.at[i]))
+
+                return 0
+
+            lax.fori_loop(0, 4, one_tile, 0)
+            o_trade(which).wait_recv()
+            edge_out[which] = ob[edge + swapped * (4 - edge)]
+            for m in (0, 1):
+                give(*o_out(which, edge, m, edge_out.at[which]))
+
+        attend(0)
+        attend(1)
 
     weights[-1].wait()
-    for h in range(heads):
-        push(back.at[h], back.at[h], fsem.at[0], bsem.at[h], blk, mate).wait_recv()
-    order = (2, 1, 3, 0)
-    for which, core in ((0, 1 - c), (1, c)):
-        for n, step in enumerate(order):
+    mates = []
+
+    def out_block(n):
+        step = order[n]
+        for h in range(heads):
+            ref = back.at[h, chunk_rows(step)]
+            push(ref, ref, fsem.at[0], bsem.at[h, (y + step) % NY], blk, mate).wait_recv()
+        for k, core in enumerate((1 - c, c)):
             u = ((y + step) % NY) * 2 + core
             for h in range(heads):
-                lhs[which, pl.ds(n * rows, rows), pl.ds(h * HD, HD)] = back[
+                lhs[n, pl.ds(k * rows, rows), pl.ds(h * HD, HD)] = back[
                     h, pl.ds(pl.multiple_of(u * rows, 16), rows), :
                 ]
-
-    part = jnp.dot(lhs[0], wo[...], preferred_element_type=jnp.float32)
-    give_mate[...] = part.astype(give_mate.dtype).reshape(give_mate.shape)
-    mates = []
-    for n in range(4):
+        part = jnp.dot(lhs[n], wo[...], preferred_element_type=jnp.float32)
+        give_mate[n] = part[:rows].astype(give_mate.dtype)
         copy = push(give_mate.at[n], from_mate.at[n], msem.at[n], mrsem.at[n], blk, mate)
         copy.start()
         mates.append(copy)
-    acc[...] = jnp.dot(lhs[1], wo[...], preferred_element_type=jnp.float32).reshape(acc.shape)
+        acc[n] = part[rows:]
 
     def cols(k):
         return slice(k * half, (k + 1) * half)
@@ -341,15 +385,13 @@
     def mixed(n, k):
         return acc[n, :, cols(k)] + from_mate[n, :, cols(k)].astype(jnp.float32)
 
-    mates[0].wait_recv()
     sent = []
-    for k, to in ((0, up), (1, dn)):
+
+    def relay(k, to):
         relay_out[k] = mixed(0, k).astype(relay_out.dtype)
         copy = push(relay_out.at[k], relay_in.at[k], ssem.at[k], rsem.at[k], blk, to)
         copy.start()
         sent.append(copy)
-    mates[1].wait_recv()
-    mates[2].wait_recv()
 
     def finish(d, k, to, extra):
         value = mixed(1 + d, k)
@@ -361,11 +403,20 @@
         copy.start()
         sent.append(copy)
 
-    for d, to in ((0, up), (1, dn)):
-        finish(d, 1 - d, to, None)
+    out_block(0)
+    out_block(1)
+    mates[0].wait_recv()
+    relay(0, up)
+    relay(1, dn)
+    mates[1].wait_recv()
+    finish(0, 1, up, None)
+    out_block(2)
+    mates[2].wait_recv()
+    finish(1, 0, dn, None)
     for d, to in ((0, up), (1, dn)):
         sent[d].wait_recv()
         finish(d, d, to, relay_in[d].astype(jnp.float32))
+    out_block(3)
     mates[3].wait_recv()
     for copy in sent[2:]:
         copy.wait_recv()
@@ -378,16 +429,20 @@
     for n in range(heads):
         for step in range(NY):
             given(*kv_out(n, step))
-        given(*q_out(n))
+            given(*q_out(n, step))
 
     @pl.when(owner)
     def _():
-        for kind in range(8):
-            tiles = 2 if kind in (RELAY_UP, RELAY_DN) else 4
+        q_trade().wait_send()
+        for kind in range(7):
+            tiles = 1 if kind in (RELAY, MATE_ACROSS) else 4
             ref = kv.at[pl.ds(0, tiles)]
             push(ref, ref, fsem.at[kind], matesem, blk, mate).wait_send()
-        for i in range(4):
-            given(*o_out(i))
+        for which in (0, 1):
+            o_trade(which).wait_send()
+            for i in range(4):
+                for m in (0, 1):
+                    given(*o_out(which, i, m, edge_out.at[which]))
 
 
 def vmem():
@@ -420,11 +475,13 @@
             pltpu.VMEM((heads * HD, width), bf16),
             pltpu.VMEM((heads, 3, TILE, HD), bf16),
             pltpu.VMEM((NX * NZ, 2, TILE, HD), bf16),
-            pltpu.VMEM((4, TILE, HD), bf16),
-            pltpu.VMEM((4, TILE, HD), bf16),
+            pltpu.VMEM((5, TILE, HD), bf16),
+            pltpu.VMEM((5, TILE // 2, HD), bf16),
+            pltpu.VMEM((5, TILE // 2, HD), bf16),
+            pltpu.VMEM((2, TILE // 2, HD), bf16),
             pltpu.VMEM((heads, TILE, HD), bf16),
-            pltpu.VMEM((WIN * WIN, TILE, TILE), f32),
-            pltpu.VMEM((2, 4 * rows, heads * HD), bf16),
+            pltpu.VMEM((WIN * WIN, TILE // 2, TILE), f32),
+            pltpu.VMEM((4, 2 * rows, heads * HD), bf16),
             pltpu.VMEM((4, rows, width), f32),
             pltpu.VMEM((4, rows, width), bf16),
             pltpu.VMEM((4, rows, width), bf16),
@@ -437,14 +494,17 @@
             dma((14,)),
             dma((8, 2)),
             dma((3, 4)),
-            dma((3,)),
+            dma((3, 4)),
             dma((NX * NZ, 4)),
-            dma((NZ, 4, 2)),
             dma,
-            dma((8,)),
+            dma((7,)),
             dma((4,)),
-            dma((3,)),
-            dma((4,)),
+            dma((3, 4)),
+            dma((2, 4, 2)),
+            dma,
+            dma,
+            dma((2,)),
+            dma((2,)),
             dma((4,)),
             dma((4,)),
             dma((6,)),

time: 86.4 us -> 81.2 us (0.940)
  Pallas kernels: 84.3 us -> 79.4 us
    pallas_call x1, Pallas kernels: 84.3 us -> 79.4 us  [on_device(): pl.pallas_call(block_kernel, out_shape=jax.ShapeDtypeStruct((rows, width)...]
where the time goes in v3:
time: 81.2 us; the launch traced here: 81.1 us
  Pallas kernels  79.4 us (98%)
  local copies, waits for them, and re-layouts  1.69 us (2%)
    pallas_call x1, Pallas kernels, on_device(): pl.pallas_call(block_kernel, out_shape=jax.ShapeDtypeStruct((rows, width)...  79.4 us
    unnamed x1, local copies, waits for them, and re-layouts  1.69 us

profile of v3, /device:TPU:1, one launch (start us, length us, event | category | flops | bytes accessed | tf_op | source)
XLA Modules:
  0.0 81.1 jit_solution(16281622874429512261)
XLA Ops:
  0.0 79.4 %block.1 = bf16[48,3072]{1,0:T(8,128)(2,1)} custom-call(s32[32]{0:T(128)} %map_ref.1, s32[2,32]{1,0:T(2,128)} %bitcast.9, bf16[48,3072]{1,0:T(8,128)(2,1)} %x_ref.1, f32[1,3072]{1,0:T(1,128)} %bitcast.6, f32[1,3072]{1,0:T(1,128)} %bitcast.7, f32[1,3072]{1,0:T(1,128)} %bitcast.8, bf16[3,3072,384]{2,1,0:T(8,128)(2,1)} %bitcast.5, bf16[384,3072]{1,0:T(8,128)(2,1)} %wo_hbm.1), custom_call_target="tpu_custom_call" | custom-call | tf_op jit(solution)/shard_map/block/pallas_call | solution.py:466
  79.4 1.7 %copy.10 = bf16[48,3072]{1,0:T(8,128)(2,1)} copy(bf16[48,3072]{1,0:T(8,128)(2,1)} %block.1) | data formatting | bytes 589824

commit v4 on v3

v4 whole, which is shorter than its diff:
```python
import jax
import jax.numpy as jnp
from jax import lax
from jax.experimental import pallas as pl
from jax.experimental.pallas import tpu as pltpu
from jax.sharding import PartitionSpec as P

TILE = 384
WIN = 3
GW = 4
NX = 4
NZ = 8
NY = 4
HD = 128
MESH = pl.DeviceIdType.MESH
VMEM_LIMIT = 62 * 1024 * 1024


def push(src, dst, send_sem, recv_sem, blk, uly):
    return pltpu.make_async_remote_copy(
        src_ref=src,
        dst_ref=dst,
        send_sem=send_sem,
        recv_sem=recv_sem,
        device_id={"blk": blk, "uly": uly},
        device_id_type=MESH,
    )


def block_kernel(
    map_ref, corner_ref, x_ref, shift_ref, scale_ref, gate_ref, w_hbm, wo_hbm, out_ref,
    xbuf, wkv, wq, wo, stage, kv, qb, ob, edge_in, edge_out, back, scores,
    lhs, acc, give_mate, from_mate, relay_out, relay_in, fin_out, fin_in,
    wsem, wosem, gsem, grsem, asem, aqsem, kvsem, matesem, fsem, qsem, bsem, osem,
    qxsem, qxrsem, oxsem, oxrsem, msem, mrsem, ssem, rsem,
):
    blk = lax.axis_index("blk")
    uly = lax.axis_index("uly")
    y, c = uly // 2, uly % 2
    x, z = blk // NZ, blk % NZ
    line = x * NZ
    rows, width = x_ref.shape
    half = width // 2
    chunk = 2 * rows
    heads = w_hbm.shape[0]
    up = ((y + 1) % NY) * 2 + c
    dn = ((y + 3) % NY) * 2 + c
    ahead = (y + 1 + 2 * c) % NY
    behind = (y + 3 + 2 * c) % NY
    onward = ahead * 2 + c
    mate = y * 2 + (1 - c)
    x_up = ((x + 1) % NX) * NZ + z
    x_dn = ((x + 3) % NX) * NZ + z
    x_far = ((x + 2) % NX) * NZ + z
    owner = z % 4 != 3
    beyond = ((x + 3 + 2 * c) % NX) * NZ + z
    edge = 3 * c

    weights = []
    for h in range(heads):
        weights.append(
            pltpu.make_async_copy(w_hbm.at[h, :, pl.ds(HD, 2 * HD)], wkv.at[h], wsem.at[h])
        )
    for h in range(heads):
        weights.append(
            pltpu.make_async_copy(
                w_hbm.at[h, :, pl.ds(0, HD)], wq.at[:, pl.ds(h * HD, HD)], wsem.at[heads + h]
            )
        )
    weights.append(pltpu.make_async_copy(wo_hbm, wo, wosem))
    for copy in weights:
        copy.start()

    peers = [(blk, mate), (blk, up), (blk, dn), (x_up, uly), (x_dn, uly), (x_far, uly), (beyond, mate)]
    for step in range(1, NZ):
        for core in (0, 1):
            peers.append((line + (z + step) % NZ, y * 2 + core))
    barrier = pltpu.get_barrier_semaphore()
    for to_blk, to_uly in peers:
        pl.semaphore_signal(
            barrier, inc=1, device_id={"blk": to_blk, "uly": to_uly}, device_id_type=MESH
        )

    values = x_ref[...].astype(jnp.float32)
    mean = jnp.mean(values, axis=-1, keepdims=True)
    centred = values - mean
    var = jnp.mean(centred * centred, axis=-1, keepdims=True)
    normed = centred * lax.rsqrt(var + 1e-06) * (1.0 + scale_ref[...]) + shift_ref[...]
    xbuf[pl.ds(pl.multiple_of(uly * rows, 16), rows), :] = normed.astype(xbuf.dtype)

    pl.semaphore_wait(barrier, len(peers))

    def piece(u, k):
        return xbuf.at[
            pl.ds(pl.multiple_of(u * rows, 16), rows), pl.ds(pl.multiple_of(k * half, 128), half)
        ]

    gathered = []

    def spread(u, k, to):
        copy = push(piece(u, k), piece(u, k), gsem.at[len(gathered)], grsem.at[u, k], blk, to)
        copy.start()
        gathered.append(copy)

    def arrive(u, k):
        push(piece(u, k), piece(u, k), gsem.at[0], grsem.at[u, k], blk, mate).wait_recv()

    def chunk_rows(step):
        return pl.ds(pl.multiple_of(((y + step) % NY) * chunk, 16), chunk)

    def blocks(stage_no):
        if stage_no in (0, 3):
            return [chunk_rows(2 if stage_no else 0)]
        return [
            pl.ds(pl.multiple_of(u * rows, 16), rows)
            for u in (((y + 3) % NY) * 2 + stage_no - 1, ((y + 1) % NY) * 2 + 2 - stage_no)
        ]

    def give(src, dst, send_sem, recv_sem, to_blk, to_uly, is_self):
        @pl.when(jnp.logical_not(is_self))
        def _():
            push(src, dst, send_sem, recv_sem, to_blk, to_uly).start()

        @pl.when(is_self)
        def _():
            pltpu.make_async_copy(src, dst, recv_sem).start()

    def given(src, dst, send_sem, recv_sem, to_blk, to_uly, is_self):
        @pl.when(jnp.logical_not(is_self))
        def _():
            push(src, dst, send_sem, recv_sem, to_blk, to_uly).wait_send()

    def turn(n):
        return (z + n) % heads

    def kv_out(n, stage_no, b):
        h = turn(n)
        zd = 4 * c + h
        core = z % 2
        at = blocks(stage_no)[b]
        return (
            stage.at[h, pl.ds(1, 2), at], kv.at[blk, :, at], asem.at[n, stage_no, b],
            kvsem.at[blk, stage_no],
            line + zd, y * 2 + core, jnp.logical_and(zd == z, core == c),
        )

    def q_out(n, stage_no, b):
        h = turn(n)
        zd = 4 * c + h
        core = z // 4
        at = blocks(stage_no)[b]
        return (
            stage.at[h, 0, at], qb.at[z % 4, at], aqsem.at[n, stage_no, b], qsem.at[z % 4],
            line + zd, y * 2 + core, jnp.logical_and(zd == z, core == c),
        )

    def gather_rows(spans):
        return jnp.concatenate([xbuf[span, :] for span in spans], axis=0)

    def project(stage_no):
        spans = blocks(stage_no)
        left = gather_rows(spans)
        for h in range(heads):
            result = jnp.dot(left, wkv[h], preferred_element_type=jnp.float32)
            for b, span in enumerate(spans):
                for part in (0, 1):
                    stage[h, 1 + part, span, :] = result[
                        b * span.size : (b + 1) * span.size, part * HD : (part + 1) * HD
                    ].astype(stage.dtype)
        for n in range(heads):
            for b in range(len(spans)):
                give(*kv_out(n, stage_no, b))

    def project_queries(stages):
        spans = [span for stage_no in stages for span in blocks(stage_no)]
        result = jnp.dot(gather_rows(spans), wq[...], preferred_element_type=jnp.float32)
        done = 0
        for span in spans:
            for h in range(heads):
                stage[h, 0, span, :] = result[
                    done : done + span.size, h * HD : (h + 1) * HD
                ].astype(stage.dtype)
            done += span.size
        for n in range(heads):
            for stage_no in stages:
                for b in range(len(blocks(stage_no))):
                    give(*q_out(n, stage_no, b))

    odd = (z + c) % 2
    mine = []
    for even_gap, odd_gap in ((0, 1), (2, 7), (6, 3), (4, 5)):
        mine.append((z + even_gap + odd * (odd_gap - even_gap)) % NZ)
    X_UP, X_DN, MATE_LINE, MATE_BELOW, MATE_ABOVE, FAR, MATE_ACROSS = range(7)

    def kv_wait(slot, stage_no):
        ref = kv.at[slot, :, chunk_rows(0)]
        push(ref, ref, fsem.at[0], kvsem.at[slot, stage_no], blk, mate).wait_recv()

    def kv_pass(slot, stage_no, kind, to_blk, to_uly, recv_sem):
        for at in blocks(stage_no):
            ref = kv.at[slot, :, at]
            push(ref, ref, fsem.at[kind], recv_sem, to_blk, to_uly).start()

    def pump_line(stage_no):
        for zs in mine:
            slot = line + zs
            kv_wait(slot, stage_no)
            kv_pass(slot, stage_no, X_UP, x_up, uly, kvsem.at[slot, stage_no])
            kv_pass(slot, stage_no, X_DN, x_dn, uly, kvsem.at[slot, stage_no])
            kv_pass(slot, stage_no, MATE_LINE, blk, mate, matesem)
        last = line + 7 * c
        kv_pass(last, stage_no, FAR, x_far, uly, kvsem.at[last, stage_no])

    def pump_sides(stage_no):
        for zs in mine:
            below = ((x + 3) % NX) * NZ + zs
            above = ((x + 1) % NX) * NZ + zs
            kv_wait(below, stage_no)
            kv_pass(below, stage_no, MATE_BELOW, blk, mate, matesem)
            kv_wait(above, stage_no)
            kv_pass(above, stage_no, MATE_ABOVE, blk, mate, matesem)

    def pump_across(stage_no):
        across = ((x + 2) % NX) * NZ + 7 * c
        kv_wait(across, stage_no)
        kv_pass(across, stage_no, MATE_ACROSS, blk, mate, matesem)

    for k in (c, 1 - c):
        spread(uly, k, onward)
        spread(uly, k, mate)
    for k in (c, 1 - c):
        arrive(mate, k)
        spread(mate, k, onward)
    for h in range(heads):
        weights[h].wait()
    project(0)
    for h in range(heads):
        weights[heads + h].wait()
    project_queries((0,))
    for stage_no, core in ((1, c), (2, 1 - c)):
        arrive(behind * 2 + core, c)
        spread(behind * 2 + core, c, onward)
        spread(behind * 2 + core, c, mate)
        arrive(behind * 2 + core, 1 - c)
        spread(behind * 2 + core, 1 - c, mate)
        for k in (1 - c, c):
            arrive(ahead * 2 + 1 - core, k)
        project(stage_no)

    @pl.when(owner)
    def _():
        pump_line(0)

    across = ((y + 2) % NY) * 2
    for core in (c, 1 - c):
        arrive(across + core, c)
        spread(across + core, c, mate)
    for core in (1 - c, c):
        arrive(across + core, 1 - c)
    project(3)
    project_queries((1, 2, 3))

    order = (2, 1, 3, 0)

    def o_out(which, i, n, src):
        core = z // 4
        h = z % 4
        to_z = 4 * c + i
        step = 2 + which if n == 0 else 1 - which + NY
        return (
            src.at[pl.ds(n * chunk, chunk)], back.at[h, chunk_rows(step)],
            osem.at[which, i, n], bsem.at[h, (y + step) % NY],
            line + to_z, y * 2 + core, jnp.logical_and(to_z == z, core == c),
        )

    def q_trade():
        return push(qb.at[edge], qb.at[4], qxsem, qxrsem, beyond, mate)

    def o_trade(which):
        return push(
            ob.at[which, edge], edge_in.at[which], oxsem.at[which], oxrsem.at[which], beyond, mate
        )

    @pl.when(owner)
    def _():
        pump_line(1)
        pump_sides(0)
        pump_line(2)
        pump_sides(1)
        pump_line(3)
        pump_sides(2)
        for i in range(4):
            push(qb.at[i], qb.at[i], fsem.at[0], qsem.at[i], blk, mate).wait_recv()
        q_trade().start()
        pump_sides(3)
        for stage_no in range(4):
            pump_across(stage_no)
        rest = kv.at[pl.ds(0, 13)]
        push(rest, rest, fsem.at[0], matesem, blk, mate).wait_recv()
        q_trade().wait_recv()

        factor = 1.0 / (HD**0.5)
        end = line + 4 * c + edge
        swapped = jnp.clip((map_ref[end] - end) * (2 * c - 1), 0, 1)

        def settle(which):
            o_trade(which).wait_recv()
            edge_out[which] = jnp.where(swapped > 0, edge_in[which], ob[which, edge])
            for m in (0, 1):
                give(*o_out(which, edge, m, edge_out.at[which]))

        def half_tile(turn_no, _):
            later = jnp.clip(turn_no - 1, 0, 1)
            which = jnp.clip(turn_no - 2, 0, 5) // 3 * later + turn_no * (1 - later)
            i = (edge + later * (1 + (turn_no + 1 + z) % 3)) % 4
            other = (1 - later) * swapped
            position = line + 4 * c + i + other * (2 * c - 1)
            row0 = corner_ref[0, position]
            col0 = corner_ref[1, position]
            at = i + other * (4 - i)
            queries = jnp.concatenate(
                [qb[at, chunk_rows(step), :] for step in (2 + which, 1 - which + NY)], axis=0
            )
            slots = []
            best = None
            for w in range(WIN * WIN):
                slot = map_ref[(row0 + w // WIN) * GW + col0 + w % WIN]
                slots.append(slot)
                s = lax.dot_general(
                    queries, kv[slot, 0], (((1,), (1,)), ((), ())),
                    preferred_element_type=jnp.float32,
                )
                scores[w] = s
                for m in range(TILE // HD):
                    part = s[:, m * HD : (m + 1) * HD]
                    best = part if best is None else jnp.maximum(best, part)
            highest = jnp.max(best, axis=-1, keepdims=True)
            total = jnp.zeros((2 * chunk, HD), jnp.float32)
            accum = jnp.zeros((2 * chunk, HD), jnp.float32)
            for w in range(WIN * WIN):
                probs = jnp.exp((scores[w] - highest) * factor)
                for m in range(TILE // HD):
                    total = total + probs[:, m * HD : (m + 1) * HD]
                accum = accum + jnp.dot(
                    probs.astype(jnp.bfloat16), kv[slots[w], 1],
                    preferred_element_type=jnp.float32,
                )
            denom = jnp.sum(total, axis=-1, keepdims=True)
            ob[which, i] = (accum / denom).astype(ob.dtype)

            @pl.when(turn_no < 2)
            def _():
                o_trade(which).start()

            @pl.when(turn_no > 1)
            def _():
                for m in (0, 1):
                    give(*o_out(which, i, m, ob.at[which, i]))

            @pl.when(turn_no == 4)
            def _():
                settle(0)

            return 0

        lax.fori_loop(0, 8, half_tile, 0)
        settle(1)

    weights[-1].wait()
    mates = []

    def out_block(n):
        step = order[n]
        for h in range(heads):
            ref = back.at[h, chunk_rows(step)]
            push(ref, ref, fsem.at[0], bsem.at[h, (y + step) % NY], blk, mate).wait_recv()
        for k, core in enumerate((1 - c, c)):
            u = ((y + step) % NY) * 2 + core
            for h in range(heads):
                lhs[n, pl.ds(k * rows, rows), pl.ds(h * HD, HD)] = back[
                    h, pl.ds(pl.multiple_of(u * rows, 16), rows), :
                ]
        part = jnp.dot(lhs[n], wo[...], preferred_element_type=jnp.float32)
        give_mate[n] = part[:rows].astype(give_mate.dtype)
        copy = push(give_mate.at[n], from_mate.at[n], msem.at[n], mrsem.at[n], blk, mate)
        copy.start()
        mates.append(copy)
        acc[n] = part[rows:]

    def cols(k):
        return slice(k * half, (k + 1) * half)

    def mixed(n, k):
        return acc[n, :, cols(k)] + from_mate[n, :, cols(k)].astype(jnp.float32)

    sent = []

    def relay(k, to):
        relay_out[k] = mixed(0, k).astype(relay_out.dtype)
        copy = push(relay_out.at[k], relay_in.at[k], ssem.at[k], rsem.at[k], blk, to)
        copy.start()
        sent.append(copy)

    def finish(d, k, to, extra):
        value = mixed(1 + d, k)
        if extra is not None:
            value = value + extra
        fin_out[d, k] = value.astype(fin_out.dtype)
        n = 2 + d * 2 + k
        copy = push(fin_out.at[d, k], fin_in.at[d, k], ssem.at[n], rsem.at[n], blk, to)
        copy.start()
        sent.append(copy)

    out_block(0)
    out_block(1)
    mates[0].wait_recv()
    relay(0, up)
    relay(1, dn)
    mates[1].wait_recv()
    finish(0, 1, up, None)
    out_block(2)
    mates[2].wait_recv()
    finish(1, 0, dn, None)
    for d, to in ((0, up), (1, dn)):
        sent[d].wait_recv()
        finish(d, d, to, relay_in[d].astype(jnp.float32))
    out_block(3)
    mates[3].wait_recv()
    for copy in sent[2:]:
        copy.wait_recv()
    for k in (0, 1):
        total = mixed(3, k) + fin_in[0, k].astype(jnp.float32) + fin_in[1, k].astype(jnp.float32)
        out_ref[:, cols(k)] = (gate_ref[:, cols(k)] * total).astype(out_ref.dtype)

    for copy in gathered + sent + mates:
        copy.wait_send()
    for n in range(heads):
        for stage_no in range(4):
            for b in range(len(blocks(stage_no))):
                given(*kv_out(n, stage_no, b))
                given(*q_out(n, stage_no, b))

    @pl.when(owner)
    def _():
        q_trade().wait_send()
        for kind in range(7):
            tiles = 1 if kind in (FAR, MATE_ACROSS) else 4
            ref = kv.at[pl.ds(0, tiles)]
            push(ref, ref, fsem.at[kind], matesem, blk, mate).wait_send()
        for which in (0, 1):
            o_trade(which).wait_send()
            for i in range(4):
                for m in (0, 1):
                    given(*o_out(which, i, m, edge_out.at[which]))


def vmem():
    return pl.BlockSpec(memory_space=pltpu.VMEM)


def hbm():
    return pl.BlockSpec(memory_space=pl.ANY)


def smem():
    return pl.BlockSpec(memory_space=pltpu.SMEM)


def on_device(tokens, mod_shift, mod_scale, out_gate, w_qkv, w_out, tile_map, window_corner):
    rows, width = tokens.shape
    heads = w_qkv.shape[1]
    bf16 = jnp.bfloat16
    f32 = jnp.float32
    dma = pltpu.SemaphoreType.DMA
    return pl.pallas_call(
        block_kernel,
        out_shape=jax.ShapeDtypeStruct((rows, width), bf16),
        in_specs=[smem(), smem(), vmem(), vmem(), vmem(), vmem(), hbm(), hbm()],
        out_specs=vmem(),
        scratch_shapes=[
            pltpu.VMEM((TILE, width), bf16),
            pltpu.VMEM((heads, width, 2 * HD), bf16),
            pltpu.VMEM((width, heads * HD), bf16),
            pltpu.VMEM((heads * HD, width), bf16),
            pltpu.VMEM((heads, 3, TILE, HD), bf16),
            pltpu.VMEM((NX * NZ, 2, TILE, HD), bf16),
            pltpu.VMEM((5, TILE, HD), bf16),
            pltpu.VMEM((2, 4, TILE // 2, HD), bf16),
            pltpu.VMEM((2, TILE // 2, HD), bf16),
            pltpu.VMEM((2, TILE // 2, HD), bf16),
            pltpu.VMEM((heads, TILE, HD), bf16),
            pltpu.VMEM((WIN * WIN, TILE // 2, TILE), f32),
            pltpu.VMEM((4, 2 * rows, heads * HD), bf16),
            pltpu.VMEM((4, rows, width), f32),
            pltpu.VMEM((4, rows, width), bf16),
            pltpu.VMEM((4, rows, width), bf16),
            pltpu.VMEM((2, rows, width // 2), bf16),
            pltpu.VMEM((2, rows, width // 2), bf16),
            pltpu.VMEM((2, 2, rows, width // 2), bf16),
            pltpu.VMEM((2, 2, rows, width // 2), bf16),
            dma((6,)),
            dma,
            dma((14,)),
            dma((8, 2)),
            dma((3, 4, 2)),
            dma((3, 4, 2)),
            dma((NX * NZ, 4)),
            dma,
            dma((7,)),
            dma((4,)),
            dma((3, 4)),
            dma((2, 4, 2)),
            dma,
            dma,
            dma((2,)),
            dma((2,)),
            dma((4,)),
            dma((4,)),
            dma((6,)),
            dma((6,)),
        ],
        compiler_params=pltpu.CompilerParams(
            collective_id=0, has_side_effects=True, vmem_limit_bytes=VMEM_LIMIT
        ),
        name="block",
    )(
        tile_map, window_corner.T, tokens, mod_shift[None, :], mod_scale[None, :],
        out_gate[None, :], jnp.transpose(w_qkv, (1, 0, 2)), w_out,
    )


def solution(mesh):
    in_specs = (
        P(("blk", "uly"), None),
        P(),
        P(),
        P(),
        P(None, "uly", None),
        P("uly", None),
        P(),
        P(),
    )
    out_specs = P(("blk", "uly"), None)
    return jax.shard_map(
        on_device, mesh=mesh, in_specs=in_specs, out_specs=out_specs, check_vma=False
    )
```

time: 81.2 us -> 79.5 us (0.979)
  Pallas kernels: 79.4 us -> 77.7 us
    pallas_call x1, Pallas kernels: 79.4 us -> 77.7 us  [on_device(): pl.pallas_call(block_kernel, out_shape=jax.ShapeDtypeStruct((rows, width)...]
where the time goes in v4:
time: 79.5 us; the launch traced here: 79.4 us
  Pallas kernels  77.7 us (98%)
  local copies, waits for them, and re-layouts  1.69 us (2%)
    pallas_call x1, Pallas kernels, on_device(): pl.pallas_call(block_kernel, out_shape=jax.ShapeDtypeStruct((rows, width)...  77.7 us
    unnamed x1, local copies, waits for them, and re-layouts  1.69 us

profile of v4, /device:TPU:1, one launch (start us, length us, event | category | flops | bytes accessed | tf_op | source)
XLA Modules:
  0.0 79.4 jit_solution(547376155069794530)
XLA Ops:
  0.0 77.7 %block.1 = bf16[48,3072]{1,0:T(8,128)(2,1)} custom-call(s32[32]{0:T(128)} %map_ref.1, s32[2,32]{1,0:T(2,128)} %bitcast.9, bf16[48,3072]{1,0:T(8,128)(2,1)} %x_ref.1, f32[1,3072]{1,0:T(1,128)} %bitcast.6, f32[1,3072]{1,0:T(1,128)} %bitcast.7, f32[1,3072]{1,0:T(1,128)} %bitcast.8, bf16[3,3072,384]{2,1,0:T(8,128)(2,1)} %bitcast.5, bf16[384,3072]{1,0:T(8,128)(2,1)} %wo_hbm.1), custom_call_target="tpu_custom_call" | custom-call | tf_op jit(solution)/shard_map/block/pallas_call | solution.py:475
  77.7 1.7 %copy.10 = bf16[48,3072]{1,0:T(8,128)(2,1)} copy(bf16[48,3072]{1,0:T(8,128)(2,1)} %block.1) | data formatting | bytes 589824

commit v5 on v4

--- a/solution.py
+++ b/solution.py
@@ -208,8 +208,9 @@
             kv_pass(slot, stage_no, X_UP, x_up, uly, kvsem.at[slot, stage_no])
             kv_pass(slot, stage_no, X_DN, x_dn, uly, kvsem.at[slot, stage_no])
             kv_pass(slot, stage_no, MATE_LINE, blk, mate, matesem)
-        last = line + 7 * c
-        kv_pass(last, stage_no, FAR, x_far, uly, kvsem.at[last, stage_no])
+        if stage_no == 3:
+            last = line + 7 * c
+            kv_pass(last, stage_no, FAR, x_far, uly, kvsem.at[last, stage_no])
 
     def pump_sides(stage_no):
         for zs in mine:
@@ -219,6 +220,9 @@
             kv_pass(below, stage_no, MATE_BELOW, blk, mate, matesem)
             kv_wait(above, stage_no)
             kv_pass(above, stage_no, MATE_ABOVE, blk, mate, matesem)
+        if stage_no < 3:
+            last = ((x + 1 + 2 * c) % NX) * NZ + 7 * c
+            kv_pass(last, stage_no, FAR, beyond, uly, kvsem.at[last, stage_no])
 
     def pump_across(stage_no):
         across = ((x + 2) % NX) * NZ + 7 * c
@@ -262,24 +266,27 @@
 
     order = (2, 1, 3, 0)
 
-    def o_out(which, i, n, src):
+    def step_of(g):
+        if isinstance(g, int):
+            return order[g]
+        return jnp.where(g == 0, 2, jnp.where(g == 1, 1, jnp.where(g == 2, 3, 0)))
+
+
+    def o_out(g, i, src):
         core = z // 4
         h = z % 4
         to_z = 4 * c + i
-        step = 2 + which if n == 0 else 1 - which + NY
+        step = step_of(g)
         return (
-            src.at[pl.ds(n * chunk, chunk)], back.at[h, chunk_rows(step)],
-            osem.at[which, i, n], bsem.at[h, (y + step) % NY],
+            src, back.at[h, chunk_rows(step)], osem.at[g, i], bsem.at[h, (y + step) % NY],
             line + to_z, y * 2 + core, jnp.logical_and(to_z == z, core == c),
         )
 
     def q_trade():
         return push(qb.at[edge], qb.at[4], qxsem, qxrsem, beyond, mate)
 
-    def o_trade(which):
-        return push(
-            ob.at[which, edge], edge_in.at[which], oxsem.at[which], oxrsem.at[which], beyond, mate
-        )
+    def o_trade(g):
+        return push(ob.at[g, edge], edge_in.at[g], oxsem.at[g], oxrsem.at[g], beyond, mate)
 
     @pl.when(owner)
     def _():
@@ -303,24 +310,24 @@
         end = line + 4 * c + edge
         swapped = jnp.clip((map_ref[end] - end) * (2 * c - 1), 0, 1)
 
-        def settle(which):
-            o_trade(which).wait_recv()
-            edge_out[which] = jnp.where(swapped > 0, edge_in[which], ob[which, edge])
-            for m in (0, 1):
-                give(*o_out(which, edge, m, edge_out.at[which]))
-
-        def half_tile(turn_no, _):
-            later = jnp.clip(turn_no - 1, 0, 1)
-            which = jnp.clip(turn_no - 2, 0, 5) // 3 * later + turn_no * (1 - later)
-            i = (edge + later * (1 + (turn_no + 1 + z) % 3)) % 4
-            other = (1 - later) * swapped
+        def settle(g):
+            o_trade(g).wait_recv()
+            edge_out[g] = jnp.where(swapped > 0, edge_in[g], ob[g, edge])
+            give(*o_out(g, edge, edge_out.at[g]))
+
+        def quarter_tile(turn_no, _):
+            past = jnp.maximum(turn_no - 1, 0)
+            r = past % 4
+            full = past // 4
+            ends = jnp.logical_or(turn_no == 0, jnp.logical_and(r == 1, full < 3))
+            g = jnp.where(turn_no == 0, 0, jnp.where(ends, full + 1, full))
+            n = jnp.where(full == 3, r, jnp.where(r == 0, 0, r - 1))
+            i = jnp.where(ends, edge, (edge + 1 + (n + z) % 3) % 4)
+            other = jnp.where(ends, 1, 0) * swapped
             position = line + 4 * c + i + other * (2 * c - 1)
             row0 = corner_ref[0, position]
             col0 = corner_ref[1, position]
-            at = i + other * (4 - i)
-            queries = jnp.concatenate(
-                [qb[at, chunk_rows(step), :] for step in (2 + which, 1 - which + NY)], axis=0
-            )
+            queries = qb[i + other * (4 - i), chunk_rows(step_of(g)), :]
             slots = []
             best = None
             for w in range(WIN * WIN):
@@ -335,8 +342,8 @@
                     part = s[:, m * HD : (m + 1) * HD]
                     best = part if best is None else jnp.maximum(best, part)
             highest = jnp.max(best, axis=-1, keepdims=True)
-            total = jnp.zeros((2 * chunk, HD), jnp.float32)
-            accum = jnp.zeros((2 * chunk, HD), jnp.float32)
+            total = jnp.zeros((chunk, HD), jnp.float32)
+            accum = jnp.zeros((chunk, HD), jnp.float32)
             for w in range(WIN * WIN):
                 probs = jnp.exp((scores[w] - highest) * factor)
                 for m in range(TILE // HD):
@@ -346,25 +353,26 @@
                     preferred_element_type=jnp.float32,
                 )
             denom = jnp.sum(total, axis=-1, keepdims=True)
-            ob[which, i] = (accum / denom).astype(ob.dtype)
-
-            @pl.when(turn_no < 2)
+            ob[g, i] = (accum / denom).astype(ob.dtype)
+
+            @pl.when(ends)
             def _():
-                o_trade(which).start()
-
-            @pl.when(turn_no > 1)
+                o_trade(g).start()
+
+            @pl.when(jnp.logical_not(ends))
             def _():
-                for m in (0, 1):
-                    give(*o_out(which, i, m, ob.at[which, i]))
-
-            @pl.when(turn_no == 4)
-            def _():
-                settle(0)
+                give(*o_out(g, i, ob.at[g, i]))
+
+            for done in range(3):
+
+                @pl.when(turn_no == 4 * done + 4)
+                def _():
+                    settle(done)
 
             return 0
 
-        lax.fori_loop(0, 8, half_tile, 0)
-        settle(1)
+        lax.fori_loop(0, 16, quarter_tile, 0)
+        settle(3)
 
     weights[-1].wait()
     mates = []
@@ -412,10 +420,10 @@
         sent.append(copy)
 
     out_block(0)
-    out_block(1)
     mates[0].wait_recv()
     relay(0, up)
     relay(1, dn)
+    out_block(1)
     mates[1].wait_recv()
     finish(0, 1, up, None)
     out_block(2)
@@ -447,11 +455,10 @@
             tiles = 1 if kind in (FAR, MATE_ACROSS) else 4
             ref = kv.at[pl.ds(0, tiles)]
             push(ref, ref, fsem.at[kind], matesem, blk, mate).wait_send()
-        for which in (0, 1):
-            o_trade(which).wait_send()
+        for g in range(4):
+            o_trade(g).wait_send()
             for i in range(4):
-                for m in (0, 1):
-                    given(*o_out(which, i, m, edge_out.at[which]))
+                given(*o_out(g, i, edge_out.at[g]))
 
 
 def vmem():
@@ -485,11 +492,11 @@
             pltpu.VMEM((heads, 3, TILE, HD), bf16),
             pltpu.VMEM((NX * NZ, 2, TILE, HD), bf16),
             pltpu.VMEM((5, TILE, HD), bf16),
-            pltpu.VMEM((2, 4, TILE // 2, HD), bf16),
-            pltpu.VMEM((2, TILE // 2, HD), bf16),
-            pltpu.VMEM((2, TILE // 2, HD), bf16),
+            pltpu.VMEM((4, 4, 2 * rows, HD), bf16),
+            pltpu.VMEM((4, 2 * rows, HD), bf16),
+            pltpu.VMEM((4, 2 * rows, HD), bf16),
             pltpu.VMEM((heads, TILE, HD), bf16),
-            pltpu.VMEM((WIN * WIN, TILE // 2, TILE), f32),
+            pltpu.VMEM((WIN * WIN, 2 * rows, TILE), f32),
             pltpu.VMEM((4, 2 * rows, heads * HD), bf16),
             pltpu.VMEM((4, rows, width), f32),
             pltpu.VMEM((4, rows, width), bf16),
@@ -509,11 +516,11 @@
             dma((7,)),
             dma((4,)),
             dma((3, 4)),
-            dma((2, 4, 2)),
+            dma((4, 4)),
             dma,
             dma,
-            dma((2,)),
-            dma((2,)),
+            dma((4,)),
+            dma((4,)),
             dma((4,)),
             dma((4,)),
             dma((6,)),

time: 79.5 us -> 84.6 us (1.064)
  Pallas kernels: 77.7 us -> 82.8 us
    pallas_call x1, Pallas kernels: 77.7 us -> 82.8 us  [on_device(): pl.pallas_call(block_kernel, out_shape=jax.ShapeDtypeStruct((rows, width)...]
where the time goes in v5:
time: 84.6 us; the launch traced here: 84.5 us
  Pallas kernels  82.8 us (98%)
  local copies, waits for them, and re-layouts  1.69 us (2%)
    pallas_call x1, Pallas kernels, on_device(): pl.pallas_call(block_kernel, out_shape=jax.ShapeDtypeStruct((rows, width)...  82.8 us
    unnamed x1, local copies, waits for them, and re-layouts  1.69 us

profile of v5, /device:TPU:1, one launch (start us, length us, event | category | flops | bytes accessed | tf_op | source)
XLA Modules:
  0.0 84.5 jit_solution(16420533702608239597)
XLA Ops:
  0.0 82.8 %block.1 = bf16[48,3072]{1,0:T(8,128)(2,1)} custom-call(s32[32]{0:T(128)} %map_ref.1, s32[2,32]{1,0:T(2,128)} %bitcast.9, bf16[48,3072]{1,0:T(8,128)(2,1)} %x_ref.1, f32[1,3072]{1,0:T(1,128)} %bitcast.6, f32[1,3072]{1,0:T(1,128)} %bitcast.7, f32[1,3072]{1,0:T(1,128)} %bitcast.8, bf16[3,3072,384]{2,1,0:T(8,128)(2,1)} %bitcast.5, bf16[384,3072]{1,0:T(8,128)(2,1)} %wo_hbm.1), custom_call_target="tpu_custom_call" | custom-call | tf_op jit(solution)/shard_map/block/pallas_call | solution.py:482
  82.8 1.7 %copy.10 = bf16[48,3072]{1,0:T(8,128)(2,1)} copy(bf16[48,3072]{1,0:T(8,128)(2,1)} %block.1) | data formatting | bytes 589824

commit v6 on v4

--- a/solution.py
+++ b/solution.py
@@ -29,7 +29,7 @@
 
 def block_kernel(
     map_ref, corner_ref, x_ref, shift_ref, scale_ref, gate_ref, w_hbm, wo_hbm, out_ref,
-    xbuf, wkv, wq, wo, stage, kv, qb, ob, edge_in, edge_out, back, scores,
+    xbuf, wkv, wq, wo, stage, kv, qb, q_in, q_now, ob, edge_in, edge_out, back, scores,
     lhs, acc, give_mate, from_mate, relay_out, relay_in, fin_out, fin_in,
     wsem, wosem, gsem, grsem, asem, aqsem, kvsem, matesem, fsem, qsem, bsem, osem,
     qxsem, qxrsem, oxsem, oxrsem, msem, mrsem, ssem, rsem,
@@ -208,8 +208,9 @@
             kv_pass(slot, stage_no, X_UP, x_up, uly, kvsem.at[slot, stage_no])
             kv_pass(slot, stage_no, X_DN, x_dn, uly, kvsem.at[slot, stage_no])
             kv_pass(slot, stage_no, MATE_LINE, blk, mate, matesem)
-        last = line + 7 * c
-        kv_pass(last, stage_no, FAR, x_far, uly, kvsem.at[last, stage_no])
+        if stage_no == 3:
+            last = line + 7 * c
+            kv_pass(last, stage_no, FAR, x_far, uly, kvsem.at[last, stage_no])
 
     def pump_sides(stage_no):
         for zs in mine:
@@ -219,6 +220,9 @@
             kv_pass(below, stage_no, MATE_BELOW, blk, mate, matesem)
             kv_wait(above, stage_no)
             kv_pass(above, stage_no, MATE_ABOVE, blk, mate, matesem)
+        if stage_no < 3:
+            last = ((x + 1 + 2 * c) % NX) * NZ + 7 * c
+            kv_pass(last, stage_no, FAR, beyond, uly, kvsem.at[last, stage_no])
 
     def pump_across(stage_no):
         across = ((x + 2) % NX) * NZ + 7 * c
@@ -258,69 +262,88 @@
     for core in (1 - c, c):
         arrive(across + core, 1 - c)
     project(3)
+
+    @pl.when(owner)
+    def _():
+        pump_line(1)
+
     project_queries((1, 2, 3))
 
     order = (2, 1, 3, 0)
 
-    def o_out(which, i, n, src):
+    def step_of(g, m):
+        return 2 + g if m == 0 else 1 - g + NY
+
+    def o_out(g, i, m, src):
         core = z // 4
         h = z % 4
         to_z = 4 * c + i
-        step = 2 + which if n == 0 else 1 - which + NY
+        step = step_of(g, m)
         return (
-            src.at[pl.ds(n * chunk, chunk)], back.at[h, chunk_rows(step)],
-            osem.at[which, i, n], bsem.at[h, (y + step) % NY],
+            src.at[pl.ds(m * chunk, chunk)], back.at[h, chunk_rows(step)],
+            osem.at[g, i, m], bsem.at[h, (y + step) % NY],
             line + to_z, y * 2 + core, jnp.logical_and(to_z == z, core == c),
         )
 
     def q_trade():
-        return push(qb.at[edge], qb.at[4], qxsem, qxrsem, beyond, mate)
-
-    def o_trade(which):
-        return push(
-            ob.at[which, edge], edge_in.at[which], oxsem.at[which], oxrsem.at[which], beyond, mate
-        )
+        return push(qb.at[edge], q_in, qxsem, qxrsem, beyond, mate)
+
+    def o_trade(g):
+        return push(ob.at[g, edge], edge_in.at[g], oxsem.at[g], oxrsem.at[g], beyond, mate)
 
     @pl.when(owner)
     def _():
-        pump_line(1)
         pump_sides(0)
         pump_line(2)
         pump_sides(1)
         pump_line(3)
         pump_sides(2)
-        for i in range(4):
+        pump_sides(3)
+        push(qb.at[edge], qb.at[edge], fsem.at[0], qsem.at[edge], blk, mate).wait_recv()
+        q_trade().start()
+        for n in range(1, 4):
+            i = (edge + n) % 4
             push(qb.at[i], qb.at[i], fsem.at[0], qsem.at[i], blk, mate).wait_recv()
-        q_trade().start()
-        pump_sides(3)
         for stage_no in range(4):
             pump_across(stage_no)
         rest = kv.at[pl.ds(0, 13)]
         push(rest, rest, fsem.at[0], matesem, blk, mate).wait_recv()
-        q_trade().wait_recv()
-
-        factor = 1.0 / (HD**0.5)
+        factor = 1.4426950408889634 / (HD**0.5)
         end = line + 4 * c + edge
         swapped = jnp.clip((map_ref[end] - end) * (2 * c - 1), 0, 1)
 
-        def settle(which):
-            o_trade(which).wait_recv()
-            edge_out[which] = jnp.where(swapped > 0, edge_in[which], ob[which, edge])
+        def settle(g):
+            o_trade(g).wait_recv()
+            edge_out[g] = jnp.where(swapped > 0, edge_in[g], ob[g, edge])
             for m in (0, 1):
-                give(*o_out(which, edge, m, edge_out.at[which]))
+                give(*o_out(g, edge, m, edge_out.at[g]))
 
         def half_tile(turn_no, _):
-            later = jnp.clip(turn_no - 1, 0, 1)
-            which = jnp.clip(turn_no - 2, 0, 5) // 3 * later + turn_no * (1 - later)
-            i = (edge + later * (1 + (turn_no + 1 + z) % 3)) % 4
-            other = (1 - later) * swapped
+            g = turn_no // 4
+            r = turn_no % 4
+            ends = r == 2 - 2 * g
+            n = jnp.where(g == 0, jnp.where(r == 3, 2, r), r - 1)
+            i = jnp.where(ends, edge, (edge + 1 + (n + z) % 3) % 4)
+            other = jnp.where(ends, 1, 0) * swapped
             position = line + 4 * c + i + other * (2 * c - 1)
             row0 = corner_ref[0, position]
             col0 = corner_ref[1, position]
-            at = i + other * (4 - i)
-            queries = jnp.concatenate(
-                [qb[at, chunk_rows(step), :] for step in (2 + which, 1 - which + NY)], axis=0
-            )
+            spans = [chunk_rows(step_of(g, m)) for m in (0, 1)]
+            for m in (0, 1):
+                q_now[pl.ds(m * chunk, chunk), :] = qb[i, spans[m], :]
+
+            @pl.when(turn_no == 2)
+            def _():
+                q_trade().wait_recv()
+
+            @pl.when(ends)
+            def _():
+                for m in (0, 1):
+                    q_now[pl.ds(m * chunk, chunk), :] = jnp.where(
+                        swapped > 0, q_in[spans[m], :], qb[edge, spans[m], :]
+                    )
+
+            queries = q_now[...]
             slots = []
             best = None
             for w in range(WIN * WIN):
@@ -338,7 +361,7 @@
             total = jnp.zeros((2 * chunk, HD), jnp.float32)
             accum = jnp.zeros((2 * chunk, HD), jnp.float32)
             for w in range(WIN * WIN):
-                probs = jnp.exp((scores[w] - highest) * factor)
+                probs = jnp.exp2((scores[w] - highest) * factor)
                 for m in range(TILE // HD):
                     total = total + probs[:, m * HD : (m + 1) * HD]
                 accum = accum + jnp.dot(
@@ -346,16 +369,16 @@
                     preferred_element_type=jnp.float32,
                 )
             denom = jnp.sum(total, axis=-1, keepdims=True)
-            ob[which, i] = (accum / denom).astype(ob.dtype)
-
-            @pl.when(turn_no < 2)
+            ob[g, i] = (accum / denom).astype(ob.dtype)
+
+            @pl.when(ends)
             def _():
-                o_trade(which).start()
-
-            @pl.when(turn_no > 1)
+                o_trade(g).start()
+
+            @pl.when(jnp.logical_not(ends))
             def _():
                 for m in (0, 1):
-                    give(*o_out(which, i, m, ob.at[which, i]))
+                    give(*o_out(g, i, m, ob.at[g, i]))
 
             @pl.when(turn_no == 4)
             def _():
@@ -412,10 +435,10 @@
         sent.append(copy)
 
     out_block(0)
-    out_block(1)
     mates[0].wait_recv()
     relay(0, up)
     relay(1, dn)
+    out_block(1)
     mates[1].wait_recv()
     finish(0, 1, up, None)
     out_block(2)
@@ -447,11 +470,11 @@
             tiles = 1 if kind in (FAR, MATE_ACROSS) else 4
             ref = kv.at[pl.ds(0, tiles)]
             push(ref, ref, fsem.at[kind], matesem, blk, mate).wait_send()
-        for which in (0, 1):
-            o_trade(which).wait_send()
+        for g in (0, 1):
+            o_trade(g).wait_send()
             for i in range(4):
                 for m in (0, 1):
-                    given(*o_out(which, i, m, edge_out.at[which]))
+                    given(*o_out(g, i, m, edge_out.at[g]))
 
 
 def vmem():
@@ -484,7 +507,9 @@
             pltpu.VMEM((heads * HD, width), bf16),
             pltpu.VMEM((heads, 3, TILE, HD), bf16),
             pltpu.VMEM((NX * NZ, 2, TILE, HD), bf16),
-            pltpu.VMEM((5, TILE, HD), bf16),
+            pltpu.VMEM((4, TILE, HD), bf16),
+            pltpu.VMEM((TILE, HD), bf16),
+            pltpu.VMEM((TILE // 2, HD), bf16),
             pltpu.VMEM((2, 4, TILE // 2, HD), bf16),
             pltpu.VMEM((2, TILE // 2, HD), bf16),
             pltpu.VMEM((2, TILE // 2, HD), bf16),

time: 79.5 us -> 76.6 us (0.964)
  Pallas kernels: 77.7 us -> 74.8 us
    pallas_call x1, Pallas kernels: 77.7 us -> 74.8 us  [on_device(): pl.pallas_call(block_kernel, out_shape=jax.ShapeDtypeStruct((rows, width)...]
where the time goes in v6:
time: 76.6 us; the launch traced here: 76.5 us
  Pallas kernels  74.8 us (98%)
  local copies, waits for them, and re-layouts  1.69 us (2%)
    pallas_call x1, Pallas kernels, on_device(): pl.pallas_call(block_kernel, out_shape=jax.ShapeDtypeStruct((rows, width)...  74.8 us
    unnamed x1, local copies, waits for them, and re-layouts  1.69 us

profile of v6, /device:TPU:1, one launch (start us, length us, event | category | flops | bytes accessed | tf_op | source)
XLA Modules:
  0.0 76.5 jit_solution(9982856353342521899)
XLA Ops:
  0.0 74.8 %block.1 = bf16[48,3072]{1,0:T(8,128)(2,1)} custom-call(s32[32]{0:T(128)} %map_ref.1, s32[2,32]{1,0:T(2,128)} %bitcast.9, bf16[48,3072]{1,0:T(8,128)(2,1)} %x_ref.1, f32[1,3072]{1,0:T(1,128)} %bitcast.6, f32[1,3072]{1,0:T(1,128)} %bitcast.7, f32[1,3072]{1,0:T(1,128)} %bitcast.8, bf16[3,3072,384]{2,1,0:T(8,128)(2,1)} %bitcast.5, bf16[384,3072]{1,0:T(8,128)(2,1)} %wo_hbm.1), custom_call_target="tpu_custom_call" | custom-call | tf_op jit(solution)/shard_map/block/pallas_call | solution.py:498
  74.8 1.7 %copy.10 = bf16[48,3072]{1,0:T(8,128)(2,1)} copy(bf16[48,3072]{1,0:T(8,128)(2,1)} %block.1) | data formatting | bytes 589824

commit v7 on v6

--- a/solution.py
+++ b/solution.py
@@ -32,7 +32,7 @@
     xbuf, wkv, wq, wo, stage, kv, qb, q_in, q_now, ob, edge_in, edge_out, back, scores,
     lhs, acc, give_mate, from_mate, relay_out, relay_in, fin_out, fin_in,
     wsem, wosem, gsem, grsem, asem, aqsem, kvsem, matesem, fsem, qsem, bsem, osem,
-    qxsem, qxrsem, oxsem, oxrsem, msem, mrsem, ssem, rsem,
+    qxsem, qxrsem, oxsem, oxrsem, msem, mrsem, ssem, rsem, mixed_out, outsem,
 ):
     blk = lax.axis_index("blk")
     uly = lax.axis_index("uly")
@@ -453,7 +453,10 @@
         copy.wait_recv()
     for k in (0, 1):
         total = mixed(3, k) + fin_in[0, k].astype(jnp.float32) + fin_in[1, k].astype(jnp.float32)
-        out_ref[:, cols(k)] = (gate_ref[:, cols(k)] * total).astype(out_ref.dtype)
+        mixed_out[:, cols(k)] = (gate_ref[:, cols(k)] * total).astype(mixed_out.dtype)
+
+    result_copy = pltpu.make_async_copy(mixed_out, out_ref, outsem)
+    result_copy.start()
 
     for copy in gathered + sent + mates:
         copy.wait_send()
@@ -476,6 +479,8 @@
                 for m in (0, 1):
                     given(*o_out(g, i, m, edge_out.at[g]))
 
+    result_copy.wait()
+
 
 def vmem():
     return pl.BlockSpec(memory_space=pltpu.VMEM)
@@ -499,7 +504,7 @@
         block_kernel,
         out_shape=jax.ShapeDtypeStruct((rows, width), bf16),
         in_specs=[smem(), smem(), vmem(), vmem(), vmem(), vmem(), hbm(), hbm()],
-        out_specs=vmem(),
+        out_specs=hbm(),
         scratch_shapes=[
             pltpu.VMEM((TILE, width), bf16),
             pltpu.VMEM((heads, width, 2 * HD), bf16),
@@ -543,6 +548,8 @@
             dma((4,)),
             dma((6,)),
             dma((6,)),
+            pltpu.VMEM((rows, width), bf16),
+            dma,
         ],
         compiler_params=pltpu.CompilerParams(
             collective_id=0, has_side_effects=True, vmem_limit_bytes=VMEM_LIMIT

time: 76.6 us -> 76.5 us (level)
  no operation moved by 1% of the time
where the time goes in v7:
time: 76.5 us; the launch traced here: 76.4 us
  Pallas kernels  74.7 us (98%)
  local copies, waits for them, and re-layouts  1.69 us (2%)
    pallas_call x1, Pallas kernels, on_device(): pl.pallas_call(block_kernel, out_shape=jax.ShapeDtypeStruct((rows, width)...  74.7 us
    unnamed x1, local copies, waits for them, and re-layouts  1.69 us

profile of v7, /device:TPU:1, one launch (start us, length us, event | category | flops | bytes accessed | tf_op | source)
XLA Modules:
  0.0 76.4 jit_solution(1772616124210731731)
XLA Ops:
  0.0 74.7 %block.1 = bf16[48,3072]{1,0:T(8,128)(2,1)} custom-call(s32[32]{0:T(128)} %map_ref.1, s32[2,32]{1,0:T(2,128)} %bitcast.9, bf16[48,3072]{1,0:T(8,128)(2,1)} %x_ref.1, f32[1,3072]{1,0:T(1,128)} %bitcast.6, f32[1,3072]{1,0:T(1,128)} %bitcast.7, f32[1,3072]{1,0:T(1,128)} %bitcast.8, bf16[3,3072,384]{2,1,0:T(8,128)(2,1)} %bitcast.5, bf16[384,3072]{1,0:T(8,128)(2,1)} %wo_hbm.1), custom_call_target="tpu_custom_call" | custom-call | tf_op jit(solution)/shard_map/block/pallas_call | solution.py:503
  74.7 1.7 %copy.10 = bf16[48,3072]{1,0:T(8,128)(2,1)} copy(bf16[48,3072]{1,0:T(8,128)(2,1)} %block.1) | data formatting | bytes 589824

commit v8 on v7

--- a/solution.py
+++ b/solution.py
@@ -435,10 +435,10 @@
         sent.append(copy)
 
     out_block(0)
+    out_block(1)
     mates[0].wait_recv()
     relay(0, up)
     relay(1, dn)
-    out_block(1)
     mates[1].wait_recv()
     finish(0, 1, up, None)
     out_block(2)

time: 76.5 us -> 76 us (level)
  no operation moved by 1% of the time
where the time goes in v8:
time: 76 us; the launch traced here: 75.9 us
  Pallas kernels  74.2 us (98%)
  local copies, waits for them, and re-layouts  1.69 us (2%)
    pallas_call x1, Pallas kernels, on_device(): pl.pallas_call(block_kernel, out_shape=jax.ShapeDtypeStruct((rows, width)...  74.2 us
    unnamed x1, local copies, waits for them, and re-layouts  1.69 us

profile of v8, /device:TPU:1, one launch (start us, length us, event | category | flops | bytes accessed | tf_op | source)
XLA Modules:
  0.0 75.9 jit_solution(1370808044289967962)
XLA Ops:
  0.0 74.2 %block.1 = bf16[48,3072]{1,0:T(8,128)(2,1)} custom-call(s32[32]{0:T(128)} %map_ref.1, s32[2,32]{1,0:T(2,128)} %bitcast.9, bf16[48,3072]{1,0:T(8,128)(2,1)} %x_ref.1, f32[1,3072]{1,0:T(1,128)} %bitcast.6, f32[1,3072]{1,0:T(1,128)} %bitcast.7, f32[1,3072]{1,0:T(1,128)} %bitcast.8, bf16[3,3072,384]{2,1,0:T(8,128)(2,1)} %bitcast.5, bf16[384,3072]{1,0:T(8,128)(2,1)} %wo_hbm.1), custom_call_target="tpu_custom_call" | custom-call | tf_op jit(solution)/shard_map/block/pallas_call | solution.py:503
  74.2 1.7 %copy.10 = bf16[48,3072]{1,0:T(8,128)(2,1)} copy(bf16[48,3072]{1,0:T(8,128)(2,1)} %block.1) | data formatting | bytes 589824
